TPU v7x, 256 devices: a whole 4x4x8 slice. The times are simulated.
256 devices in a mesh: fx: 32 (over z, x), fy: 8 (over y, core).
Axes of the slice: x: 4, y: 4, z: 8, core: 2. Of those that a mesh axis runs over, the one named last changes fastest.
Arguments:
- right_side: float32 [4096, 2048], P(('fx', 'fy'))
- coupling: float32 [4096, 11, 4096], P(('fx', 'fy')), may hold values from -0.109375 to 0.109375
- face_columns: int32 [4096, 11], P(('fx', 'fy')), may hold values from 0 to 31, as said below
- ghost_lists: int32 [1024, 4], P(('fx', 'fy')), may hold values from 0 to 15, as said below
Outputs:
- solution: float32 [4096, 2048], P(('fx', 'fy'))
- residual: float32 [4096, 2048], P(('fx', 'fy'))
Inputs may be any that keep to these rules, and one draw needn't show every extreme that they name: face_columns[f, 0] is f's own index within its block; entries 1 to 6 name other faces of the same block, all distinct and below 16; entries 7 to 10 are distinct and name received faces, 16 + d * 4 + g for the g-th face of group d of the extended list; every received slot of every block is named by some row of that block. `ghost_lists`: each row names 4 distinct faces of its block by local index.
All inputs are finite; a program needn't handle non-finite values.
Results may differ from a plain program's by a relative error of at most 0.0003.
Values sent between devices are 32-bit elements; how exact they have to be, the bound alone decides.
No kernel may reach another device: no remote copies, remote signals or barrier semaphores. Data moves between devices by JAX's collectives and lax.ppermute only.
A program may use at most 64 MiB of HBM per device.

v0:
```python
import jax
import jax.numpy as jnp
from jax import lax
from jax.sharding import PartitionSpec as P

DOF = 64
NRHS = 32
BLOCKS = 11
POWERS = 3


def from_behind(block, axis, distance):
    devices = range(lax.axis_size(axis))
    route = [(i - distance, i) for i in devices if i - distance in devices]
    return lax.ppermute(block, axis, route)


def receive_rows(field, ghost_lists):
    from_lower_x = from_behind(jnp.take(field, ghost_lists[1], axis=0), "fx", 1)
    from_upper_x = from_behind(jnp.take(field, ghost_lists[0], axis=0), "fx", -1)
    from_lower_y = from_behind(jnp.take(field, ghost_lists[3], axis=0), "fy", 1)
    from_upper_y = from_behind(jnp.take(field, ghost_lists[2], axis=0), "fy", -1)
    return jnp.concatenate([from_lower_x, from_upper_x, from_lower_y, from_upper_y], axis=0)


def contract(block_mats, picked):
    face_count = picked.shape[0]
    shaped = picked.reshape(face_count, picked.shape[1], DOF, NRHS)
    result = jnp.einsum("fkab,fkbr->far", block_mats, shaped, precision=lax.Precision.HIGHEST)
    return result.reshape(face_count, DOF * NRHS)


def solve_small(gram_total):
    count = NRHS
    row_ids = jnp.arange((POWERS + 1) * count)[:, None]
    col_ids = jnp.arange(POWERS * count)[None, :]
    shift_map = ((row_ids == col_ids) | (row_ids == col_ids + count)).astype(jnp.float32)
    first = (row_ids == jnp.arange(count)[None, :]).astype(jnp.float32)
    high = lax.Precision.HIGHEST
    normal_matrix = jnp.dot(
        shift_map.T, jnp.dot(gram_total, shift_map, precision=high), precision=high
    )
    right_terms = jnp.dot(shift_map.T, gram_total[:, :count], precision=high)
    factor = jnp.linalg.cholesky(normal_matrix)
    coeffs = jax.scipy.linalg.cho_solve((factor, True), right_terms)
    combo = first - jnp.dot(shift_map, coeffs, precision=high)
    return (coeffs, combo)


def on_device(right_side, coupling, face_columns, ghost_lists):
    face_count = right_side.shape[0]
    block_mats = coupling.reshape(face_count, BLOCKS, DOF, DOF)
    high = lax.Precision.HIGHEST

    def as_rows(field):
        return field.reshape(face_count * DOF, NRHS)

    fields = [right_side]
    for power_index in range(POWERS):
        power_field = fields[-1]
        received = receive_rows(power_field, ghost_lists)
        extended = jnp.concatenate([power_field, received], axis=0)
        fields.append(contract(block_mats, jnp.take(extended, face_columns, axis=0)))
    stacked = jnp.concatenate([as_rows(item) for item in fields], axis=1)
    local_gram = jnp.dot(stacked.T, stacked, precision=high, preferred_element_type=jnp.float32)
    gram_total = lax.psum(local_gram, ("fx", "fy"))
    coeffs, combo = solve_small(gram_total)
    solution = jnp.dot(stacked[:, : POWERS * NRHS], coeffs, precision=high)
    residual = jnp.dot(stacked, combo, precision=high)
    return (solution.reshape(face_count, DOF * NRHS), residual.reshape(face_count, DOF * NRHS))


def solution(mesh):
    placed = (
        P(("fx", "fy"), None),
        P(("fx", "fy"), None, None),
        P(("fx", "fy"), None),
        P(("fx", "fy"), None),
    )
    return jax.shard_map(
        on_device,
        mesh=mesh,
        in_specs=placed,
        out_specs=(P(("fx", "fy"), None), P(("fx", "fy"), None)),
        check_vma=False,
    )
```

profile of v0, /device:TPU:8, one launch (start us, length us, event | category | flops | bytes accessed | tf_op | source)
XLA Modules:
  0.0 413.1 jit_solution(4617153673329050650)
XLA Ops:
  9.6 3.4 collective-permute-start
  17.5 1.9 collective-permute-start.2
  21.0 3.6 collective-permute-start.3
  26.2 5.7 %reshape.61 = f32[16,11,64,64]{3,2,0,1:T(8,128)} reshape(f32[16,11,4096]{2,0,1:T(8,128)} %param.9) | data formatting | bytes 5767168 | tf_op jit(solution)/shard_map/reshape | solution.py:52
  34.7 1.8 broadcast_select_fusion.2
  36.5 3.6 reshape.245
  40.0 12.0 %fusion.6 = f32[16,64,32]{1,2,0:T(8,128)S(1)} fusion(f32[16,11,64,64]{3,2,0,1:T(8,128)} %reshape.61, f32[16,11,64,32]{3,2,1,0:T(8,128)} %reshape.245), kind=kOutput, calls=%fused_computation.21 | convolution fusion | flops 276824064 | bytes 4456448 | tf_op jit(solution)/shard_map/fkab,fkbr->far/dot_general | solution.py:29
  56.2 1.9 collective-permute-start.6
  58.2 3.6 collective-permute-start.7
  61.9 5.3 %collective-permute-start.4 = (f32[4,2048]{1,0:T(4,128)S(1)}, f32[4,2048]{1,0:T(4,128)S(1)}, u32[]{:S(2)}, u32[]{:S(2)}) collective-permute-start(f32[4,2048]{1,0:T(4,128)S(1)} %broadcast_select_fusion.10), channel_id=1, source_target_pairs={{0,8},{8,16},{16,24},{24,32},{32,40},{40,48},{48,56},{56,64},{64,7... | collective-permute-start | bytes 98312 | tf_op jit(solution)/shard_map/ppermute | solution.py:15
  69.9 1.6 reshape.229
  71.6 3.2 broadcast_select_fusion.1
  74.8 5.2 %reshape.246 = f32[16,11,64,32]{3,2,1,0:T(8,128)} reshape(f32[16,11,2048]{2,1,0:T(8,128)} %broadcast_select_fusion.1) | data formatting | bytes 2883584 | tf_op jit(solution)/shard_map/reshape | solution.py:28
  80.0 12.0 %fusion.9 = f32[16,64,32]{1,2,0:T(8,128)S(1)} fusion(f32[16,11,64,64]{3,2,0,1:T(8,128)} %reshape.61, f32[16,11,64,32]{3,2,1,0:T(8,128)} %reshape.246), kind=kOutput, calls=%fused_computation.22 | convolution fusion | flops 276824064 | bytes 4456448 | tf_op jit(solution)/shard_map/fkab,fkbr->far/dot_general | solution.py:29
  94.8 1.9 collective-permute-start.10
  96.8 3.6 collective-permute-start.11
  101.9 5.1 %collective-permute-start.8 = (f32[4,2048]{1,0:T(4,128)S(1)}, f32[4,2048]{1,0:T(4,128)S(1)}, u32[]{:S(2)}, u32[]{:S(2)}) collective-permute-start(f32[4,2048]{1,0:T(4,128)S(1)} %broadcast_select_fusion.6), channel_id=1, source_target_pairs={{0,8},{8,16},{16,24},{24,32},{32,40},{40,48},{48,56},{56,64},{64,7... | collective-permute-start | bytes 98312 | tf_op jit(solution)/shard_map/ppermute | solution.py:15
  111.2 3.2 broadcast_select_fusion
  114.5 5.2 %reshape.247 = f32[16,11,64,32]{3,2,1,0:T(8,128)} reshape(f32[16,11,2048]{2,1,0:T(8,128)} %broadcast_select_fusion) | data formatting | bytes 2883584 | tf_op jit(solution)/shard_map/reshape | solution.py:28
  119.6 12.3 %fusion.12 = f32[16,64,32]{1,2,0:T(8,128)S(1)} fusion(f32[16,11,64,64]{3,2,0,1:T(8,128)} %reshape.61, f32[16,11,64,32]{3,2,1,0:T(8,128)} %reshape.247), kind=kOutput, calls=%fused_computation.23 | convolution fusion | flops 276824064 | bytes 4456448 | tf_op jit(solution)/shard_map/fkab,fkbr->far/dot_general | solution.py:29
  132.6 1.6 fusion.37
  134.3 248.3 %all-reduce.2.cloned.1.call-done = f32[128,128]{1,0:T(8,128)} async-done(((f32[128,128]{1,0:T(8,128)}), f32[128,128]{1,0:T(8,128)}) %all-reduce.2.cloned.1.call-update) | async-done | bytes 65552 | tf_op jit(solution)/shard_map/psum | solution.py:66
  383.9 8.8 %cholesky.16 = f32[96,96]{1,0:T(8,128)S(1)} custom-call(f32[96,96]{1,0:T(8,128)S(1)} %fusion.29), custom_call_target="Cholesky" | custom-call | tf_op jit(solution)/shard_map/jit(cholesky)/cholesky | solution.py:44
  394.1 7.4 %custom-call.10 = f32[1,96,96]{1,2,0:T(8,128)S(1)} custom-call(f32[1,96,96]{2,1,0:T(8,128)S(1)} %fusion.24), custom_call_target="InvertDiagBlocksLowerTriangular" | custom-call | tf_op jit(solution)/shard_map/jit(_cho_solve)/triangular_solve | solution.py:45
  (83 shorter events, 36.4 us)
Async XLA Ops:
  7.2 375.4 %all-reduce.2.cloned.1.call-start = ((), (), s32[]{:S(2)}) async-start(), calls=%async_computation | async-start | bytes 131072 | tf_op jit(solution)/shard_map/psum | solution.py:66
  9.6 22.2 %collective-permute-start = (f32[4,2048]{1,0:T(4,128)S(1)}, f32[4,2048]{1,0:T(4,128)S(1)}, u32[]{:S(2)}, u32[]{:S(2)}) collective-permute-start(f32[4,2048]{1,0:T(4,128)S(1)} %broadcast_select_fusion.14), channel_id=1, source_target_pairs={{0,8},{8,16},{16,24},{24,32},{32,40},{40,48},{48,56},{56,64},{64,7... | collective-permute-start | bytes 98312 | tf_op jit(solution)/shard_map/ppermute | solution.py:15
  14.6 17.2 %collective-permute-start.1 = (f32[4,2048]{1,0:T(4,128)S(1)}, f32[4,2048]{1,0:T(4,128)S(1)}, u32[]{:S(2)}, u32[]{:S(2)}) collective-permute-start(f32[4,2048]{1,0:T(4,128)S(1)} %broadcast_select_fusion.13), channel_id=1, source_target_pairs={{8,0},{16,8},{24,16},{32,24},{40,32},{48,40},{56,48},{64,56},{72,6... | collective-permute-start | bytes 98312 | tf_op jit(solution)/shard_map/ppermute | solution.py:15
  17.5 14.4 %collective-permute-start.2 = (f32[4,2048]{1,0:T(4,128)S(1)}, f32[4,2048]{1,0:T(4,128)S(1)}, u32[]{:S(2)}, u32[]{:S(2)}) collective-permute-start(f32[4,2048]{1,0:T(4,128)S(1)} %broadcast_select_fusion.12), channel_id=1, source_target_pairs={{0,1},{1,2},{2,3},{3,4},{4,5},{5,6},{6,7},{8,9},{9,10},{10,11},{11... | collective-permute-start | bytes 98312 | tf_op jit(solution)/shard_map/ppermute | solution.py:15
  21.0 10.9 %collective-permute-start.3 = (f32[4,2048]{1,0:T(4,128)S(1)}, f32[4,2048]{1,0:T(4,128)S(1)}, u32[]{:S(2)}, u32[]{:S(2)}) collective-permute-start(f32[4,2048]{1,0:T(4,128)S(1)} %broadcast_select_fusion.11), channel_id=1, source_target_pairs={{1,0},{2,1},{3,2},{4,3},{5,4},{6,5},{7,6},{9,8},{10,9},{11,10},{12... | collective-permute-start | bytes 98312 | tf_op jit(solution)/shard_map/ppermute | solution.py:15
  26.1 5.7 %copy-start = (f32[16,2048]{1,0:T(8,128)S(1)}, f32[16,2048]{1,0:T(8,128)}, u32[]{:S(2)}) copy-start(f32[16,2048]{1,0:T(8,128)} %param.8) | copy-start | bytes 393220
  54.9 12.4 %collective-permute-start.5 = (f32[4,2048]{1,0:T(4,128)S(1)}, f32[4,2048]{1,0:T(4,128)S(1)}, u32[]{:S(2)}, u32[]{:S(2)}) collective-permute-start(f32[4,2048]{1,0:T(4,128)S(1)} %broadcast_select_fusion.9), channel_id=1, source_target_pairs={{8,0},{16,8},{24,16},{32,24},{40,32},{48,40},{56,48},{64,56},{72,6... | collective-permute-start | bytes 98312 | tf_op jit(solution)/shard_map/ppermute | solution.py:15
  56.2 11.1 %collective-permute-start.6 = (f32[4,2048]{1,0:T(4,128)S(1)}, f32[4,2048]{1,0:T(4,128)S(1)}, u32[]{:S(2)}, u32[]{:S(2)}) collective-permute-start(f32[4,2048]{1,0:T(4,128)S(1)} %broadcast_select_fusion.8), channel_id=1, source_target_pairs={{0,1},{1,2},{2,3},{3,4},{4,5},{5,6},{6,7},{8,9},{9,10},{10,11},{11... | collective-permute-start | bytes 98312 | tf_op jit(solution)/shard_map/ppermute | solution.py:15
  58.2 9.1 %collective-permute-start.7 = (f32[4,2048]{1,0:T(4,128)S(1)}, f32[4,2048]{1,0:T(4,128)S(1)}, u32[]{:S(2)}, u32[]{:S(2)}) collective-permute-start(f32[4,2048]{1,0:T(4,128)S(1)} %broadcast_select_fusion.7), channel_id=1, source_target_pairs={{1,0},{2,1},{3,2},{4,3},{5,4},{6,5},{7,6},{9,8},{10,9},{11,10},{12... | collective-permute-start | bytes 98312 | tf_op jit(solution)/shard_map/ppermute | solution.py:15
  61.9 6.8 %collective-permute-start.4 = (f32[4,2048]{1,0:T(4,128)S(1)}, f32[4,2048]{1,0:T(4,128)S(1)}, u32[]{:S(2)}, u32[]{:S(2)}) collective-permute-start(f32[4,2048]{1,0:T(4,128)S(1)} %broadcast_select_fusion.10), channel_id=1, source_target_pairs={{0,8},{8,16},{16,24},{24,32},{32,40},{40,48},{48,56},{56,64},{64,7... | collective-permute-start | bytes 98312 | tf_op jit(solution)/shard_map/ppermute | solution.py:15
  94.8 12.3 %collective-permute-start.10 = (f32[4,2048]{1,0:T(4,128)S(1)}, f32[4,2048]{1,0:T(4,128)S(1)}, u32[]{:S(2)}, u32[]{:S(2)}) collective-permute-start(f32[4,2048]{1,0:T(4,128)S(1)} %broadcast_select_fusion.4), channel_id=1, source_target_pairs={{0,1},{1,2},{2,3},{3,4},{4,5},{5,6},{6,7},{8,9},{9,10},{10,11},{11... | collective-permute-start | bytes 98312 | tf_op jit(solution)/shard_map/ppermute | solution.py:15
  96.8 10.3 %collective-permute-start.11 = (f32[4,2048]{1,0:T(4,128)S(1)}, f32[4,2048]{1,0:T(4,128)S(1)}, u32[]{:S(2)}, u32[]{:S(2)}) collective-permute-start(f32[4,2048]{1,0:T(4,128)S(1)} %broadcast_select_fusion.3), channel_id=1, source_target_pairs={{1,0},{2,1},{3,2},{4,3},{5,4},{6,5},{7,6},{9,8},{10,9},{11,10},{12... | collective-permute-start | bytes 98312 | tf_op jit(solution)/shard_map/ppermute | solution.py:15
  100.6 6.6 %collective-permute-start.9 = (f32[4,2048]{1,0:T(4,128)S(1)}, f32[4,2048]{1,0:T(4,128)S(1)}, u32[]{:S(2)}, u32[]{:S(2)}) collective-permute-start(f32[4,2048]{1,0:T(4,128)S(1)} %broadcast_select_fusion.5), channel_id=1, source_target_pairs={{8,0},{16,8},{24,16},{32,24},{40,32},{48,40},{56,48},{64,56},{72,6... | collective-permute-start | bytes 98312 | tf_op jit(solution)/shard_map/ppermute | solution.py:15
  101.9 6.4 %collective-permute-start.8 = (f32[4,2048]{1,0:T(4,128)S(1)}, f32[4,2048]{1,0:T(4,128)S(1)}, u32[]{:S(2)}, u32[]{:S(2)}) collective-permute-start(f32[4,2048]{1,0:T(4,128)S(1)} %broadcast_select_fusion.6), channel_id=1, source_target_pairs={{0,8},{8,16},{16,24},{24,32},{32,40},{40,48},{48,56},{56,64},{64,7... | collective-permute-start | bytes 98312 | tf_op jit(solution)/shard_map/ppermute | solution.py:15
Sparse Core Ops, SparseCore 0:
  134.4 248.1 all-reduce.1
where the time goes:
time: 416 us; the launch traced here: 413 us
  waiting for transfers between devices  251 us (60%)
  matrix products  42.2 us (10%)
  local copies, waits for them, and re-layouts  41.9 us (10%)
  starting transfers between devices  34.3 us (8%)
  other arithmetic  29.4 us (7%)
  between operations  14.5 us (3%)
    psum x1, waiting for transfers between devices, on_device(): gram_total = lax.psum(local_gram, ('fx', 'fy'))  248 us
    dot_general x3, matrix products, contract(): jnp.einsum('fkab,fkbr->far', block_mats, shaped, precision=lax.Precision....  36.3 us
    ppermute x12, starting transfers between devices, from_behind(): return lax.ppermute(block, axis, route)  34.3 us
    reshape x3, local copies, waits for them, and re-layouts, contract(): shaped = picked.reshape(face_count, picked.shape[1], DOF, NRHS)  13.9 us
    another operation x3, other arithmetic, solve_small(): factor = jnp.linalg.cholesky(normal_matrix)  9.45 us
    select_n x4, other arithmetic, on_device(): jnp.take(extended, face_columns, axis=0)  8.94 us
  transfers between devices with their start and end apart: 13, of which 3 were waited for; matrix products, arithmetic and copies ran while one was open for 3% of the time, Pallas kernels for 0%

commit v1 on v0

v1 whole, which is shorter than its diff:
```python
import functools

import jax
import jax.numpy as jnp
from jax import lax
from jax.experimental import pallas as pl
from jax.experimental.pallas import tpu as pltpu
from jax.sharding import PartitionSpec as P

DOF = 64
NRHS = 32
BLOCKS = 11
OWNED = 7
POWERS = 3
FACE_DEV = 16
GHOST = 4
LANES = 128
COPIES = LANES // NRHS
ROWS = FACE_DEV * DOF
OWN_DEPTH = 512
GHOST_DEPTH = 256
SYSTEM = POWERS * NRHS

VMEM = pl.BlockSpec(memory_space=pltpu.VMEM)
SMEM = pl.BlockSpec(memory_space=pltpu.SMEM)
F32 = jnp.float32
BF16 = jnp.bfloat16


def shape_of(rows, columns, dtype=F32):
    return jax.ShapeDtypeStruct((rows, columns), dtype)


def lane_group(rows):
    return lax.broadcasted_iota(jnp.int32, (rows, LANES), 1) // NRHS


def by_group(group, parts):
    low = jnp.where(group == 0, parts[0], parts[1])
    high = jnp.where(group == 2, parts[2], parts[3])
    return jnp.where(group < 2, low, high)


def spread(tile):
    group = lane_group(tile.shape[0])
    turned = [tile] + [pltpu.roll(tile, NRHS * s, 1) for s in range(1, COPIES)]
    return [by_group(group, [turned[(c - j) % COPIES] for c in range(COPIES)]) for j in range(COPIES)]


def high_low(field):
    group = lane_group(field.shape[0])
    high = field.astype(BF16).astype(F32)
    return jnp.where(group % 2 == 0, high, field - high).astype(BF16)


def first_directions():
    odd_x = lax.rem(lax.axis_index("fx"), 2)
    odd_y = lax.rem(lax.axis_index("fy"), 2)
    return (1 - odd_x, odd_x, 3 - odd_y, 2 + odd_y)


def inside(direction):
    fx, fy = lax.axis_index("fx"), lax.axis_index("fy")
    last_x, last_y = lax.axis_size("fx") - 1, lax.axis_size("fy") - 1
    out = (direction == 0) & (fx == 0) | (direction == 1) & (fx == last_x)
    return jnp.logical_not(out | (direction == 2) & (fy == 0) | (direction == 3) & (fy == last_y))


def write_sends(lists, field_ref, send_refs):
    group = lane_group(FACE_DEV)
    for direction, send_ref in zip(first_directions(), send_refs):
        for g in range(GHOST):
            start = lists[direction, g] * DOF
            parts = [field_ref[pl.ds(start + j, FACE_DEV, stride=COPIES), :] for j in range(COPIES)]
            send_ref[g * FACE_DEV : (g + 1) * FACE_DEV, :] = by_group(group, parts)


def spread_kernel(lists, right_ref, field_ref, *send_refs):
    for t in range(DOF // COPIES):
        parts = spread(right_ref[:, t * LANES : (t + 1) * LANES])
        for j in range(COPIES):
            field_ref[pl.ds(COPIES * t + j, FACE_DEV, stride=DOF), :] = parts[j]
    write_sends(lists, field_ref, send_refs)


def weights_kernel(coupling_ref, own_high, own_low, ghost_high, ghost_low):
    rows = own_high.shape[2]
    left = lax.broadcasted_iota(jnp.int32, (rows, LANES), 1) < DOF
    zero = jnp.zeros((rows, LANES), F32)
    order = list(range(OWNED)) + [None] + list(range(OWNED, BLOCKS))
    for face in range(own_high.shape[0]):
        tiles = [zero if k is None else coupling_ref[k, pl.ds(face, rows, stride=8), :] for k in order]
        turned = [zero if k is None else pltpu.roll(tile, DOF, 1) for k, tile in zip(order, tiles)]
        for q in range(len(order) // 2):
            even = jnp.where(left, tiles[2 * q], turned[2 * q + 1])
            odd = jnp.where(left, turned[2 * q], tiles[2 * q + 1])
            if q < OWN_DEPTH // LANES:
                high_ref, low_ref, lane = own_high, own_low, q * LANES
            else:
                high_ref, low_ref, lane = ghost_high, ghost_low, q * LANES - OWN_DEPTH
            for s, part in ((0, even), (1, odd)):
                high = part.astype(BF16)
                high_ref[face, s, :, lane : lane + LANES] = high
                low_ref[face, s, :, lane : lane + LANES] = (part - high.astype(F32)).astype(BF16)


def product(high_ref, low_ref, face, picked):
    depth = picked.shape[0]
    high = high_ref[face].reshape(DOF, depth)
    low = low_ref[face].reshape(DOF, depth)
    both = jnp.dot(high, picked, preferred_element_type=F32)
    both = both + jnp.dot(low, picked, preferred_element_type=F32)
    return both + pltpu.roll(both, NRHS, 1)


def pick(rows_ref, numbers):
    starts = [pl.multiple_of(number * DOF, DOF) for number in numbers]
    return jnp.concatenate([rows_ref[pl.ds(start, DOF), :] for start in starts], axis=0)


def own_kernel(columns, field_ref, high_ref, low_ref, sum_ref, split_ref):
    for face in range(FACE_DEV):
        at = slice(face * DOF, (face + 1) * DOF)
        split_ref[at, :] = high_low(field_ref[at, :])
    for face in range(FACE_DEV):
        numbers = [columns[face, k] for k in range(OWNED)]
        picked = pick(split_ref, numbers + numbers[:1])
        sum_ref[face * DOF : (face + 1) * DOF, :] = product(high_ref, low_ref, face, picked)


def add_ghosts(columns, received, sum_ref, high_ref, low_ref, field_ref, spread_ref, split_ref):
    for direction, received_ref in zip(first_directions(), received):
        keep = inside(direction)
        for g in range(GHOST):
            tile = received_ref[g * FACE_DEV : (g + 1) * FACE_DEV, :]
            parts = spread(jnp.where(keep, tile, 0.0))
            start = (direction * GHOST + g) * DOF
            for j in range(COPIES):
                spread_ref[pl.ds(start + j, FACE_DEV, stride=COPIES), :] = parts[j]
    for slot in range(4 * GHOST):
        at = slice(slot * DOF, (slot + 1) * DOF)
        split_ref[at, :] = high_low(spread_ref[at, :])
    for face in range(FACE_DEV):
        picked = pick(split_ref, [columns[face, k] - FACE_DEV for k in range(OWNED, BLOCKS)])
        total = sum_ref[face * DOF : (face + 1) * DOF, :] + product(high_ref, low_ref, face, picked)
        for s in range(2):
            rows = pl.ds(face * DOF + s, DOF // 2, stride=2)
            field_ref[rows, :] = total[s * DOF // 2 : (s + 1) * DOF // 2, :]


def ghost_kernel(columns, lists, r0, r1, r2, r3, sum_ref, high_ref, low_ref, field_ref, s0, s1, s2, s3, spread_ref, split_ref):
    add_ghosts(columns, (r0, r1, r2, r3), sum_ref, high_ref, low_ref, field_ref, spread_ref, split_ref)
    write_sends(lists, field_ref, (s0, s1, s2, s3))


def last_kernel(
    columns, r0, r1, r2, r3, sum_ref, high_ref, low_ref, f0, f1, f2, system_ref, basis_ref, f3, spread_ref, split_ref
):
    add_ghosts(columns, (r0, r1, r2, r3), sum_ref, high_ref, low_ref, f3, spread_ref, split_ref)
    group = lane_group(LANES)
    gram = jnp.zeros((LANES, 2 * LANES), F32)
    for part in range(ROWS // LANES):
        at = slice(part * LANES, (part + 1) * LANES)
        basis = by_group(group, [ref[at, :] for ref in (f0, f1, f2, f3)])
        high = basis.astype(BF16)
        low = (basis - high.astype(F32)).astype(BF16)
        both = jnp.concatenate([high, low], axis=1)
        basis_ref[at, :] = both
        gram = gram + lax.dot_general(high, both, (((0,), (0,)), ((), ())), preferred_element_type=F32)
    cross = gram[:, LANES:]
    full = gram[:, :LANES] + cross + cross.T
    pairs = full[:SYSTEM] + full[NRHS:]
    lane = lax.broadcasted_iota(jnp.int32, (SYSTEM, LANES), 1)
    system_ref[...] = pltpu.roll(pairs, SYSTEM, 1) + jnp.where(lane < SYSTEM, pairs, 0.0)


def finish_kernel(mine, other, basis_ref, solution_ref, residual_ref, out_ref):
    system = mine[...] + other[...]
    row = lax.broadcasted_iota(jnp.int32, (SYSTEM, LANES), 0)
    for j in range(SYSTEM):
        line = system[j : j + 1, :]
        line = line / line[:, j : j + 1]
        factor = jnp.where(row == j, 0.0, system[:, j : j + 1])
        system = jnp.where(row == j, line, system) - factor * line
    lane = lax.broadcasted_iota(jnp.int32, (SYSTEM, LANES), 1)
    coeffs = jnp.where(lane >= SYSTEM, system, 0.0)
    coeffs = coeffs + pltpu.roll(coeffs, NRHS, 1)
    coeffs = coeffs + pltpu.roll(coeffs, 2 * NRHS, 1)
    zero = jnp.zeros((NRHS, LANES), F32)
    first_row = lax.broadcasted_iota(jnp.int32, (LANES, LANES), 0)
    first_lane = lax.broadcasted_iota(jnp.int32, (LANES, LANES), 1)
    first = jnp.where(first_row == first_lane % NRHS, 1.0, 0.0)
    padded = jnp.concatenate([coeffs, zero], axis=0)
    combo = first - (padded + jnp.concatenate([zero, coeffs], axis=0))
    both = jnp.concatenate([padded, combo], axis=1)
    high = both.astype(BF16)
    low = (both - high.astype(F32)).astype(BF16)
    twice = jnp.concatenate([high, high], axis=0)
    for part in range(ROWS // LANES):
        at = slice(part * LANES, (part + 1) * LANES)
        out = jnp.dot(basis_ref[at, :], twice, preferred_element_type=F32)
        out = out + jnp.dot(basis_ref[at, :LANES], low, preferred_element_type=F32)
        out_ref[0, at, :] = out[:, :LANES]
        out_ref[1, at, :] = out[:, LANES:]
    group = lane_group(FACE_DEV)
    for t in range(DOF // COPIES):
        for side, result_ref in ((0, solution_ref), (1, residual_ref)):
            parts = [out_ref[side, pl.ds(COPIES * t + j, FACE_DEV, stride=DOF), :] for j in range(COPIES)]
            result_ref[:, t * LANES : (t + 1) * LANES] = by_group(group, parts)


def pairs_of(size, second):
    if not second:
        return [(i, i ^ 1) for i in range(size)]
    ahead = [(i, (i + 1) % size) for i in range(1, size, 2)]
    return ahead + [(b, a) for a, b in ahead]


def exchange(sends):
    routes = (("fx", False), ("fx", True), ("fy", False), ("fy", True))
    return [
        lax.ppermute(send, axis, pairs_of(lax.axis_size(axis), second))
        for send, (axis, second) in zip(sends, routes)
    ]


ROUNDS = (("fy", (1,)), ("fy", (2, 4, 6)), ("fx", (1, 2, 3)), ("fx", (4, 8, 12)))
LAST_ROUND = ("fx", 16)


def from_partner(part, axis, distance):
    return lax.ppermute(part, axis, [(i, i ^ distance) for i in range(lax.axis_size(axis))])


def add_over_devices(part):
    for axis, distances in ROUNDS:
        others = [from_partner(part, axis, d) for d in distances]
        part = part + others[0]
        if len(others) == 3:
            part = part + (others[1] + others[2])
    return part, from_partner(part, *LAST_ROUND)


def params(**extra):
    return dict(compiler_params=pltpu.CompilerParams(vmem_limit_bytes=40 << 20, **extra))


def on_device(right_side, coupling, face_columns, ghost_lists):
    send = shape_of(GHOST * FACE_DEV, LANES)
    field_shape = shape_of(ROWS, LANES)
    outs = pl.pallas_call(
        spread_kernel,
        out_shape=[field_shape] + [send] * 4,
        in_specs=[SMEM, VMEM],
        out_specs=[VMEM] * 5,
        name="spread",
        **params(),
    )(ghost_lists, right_side)
    fields, sends = [outs[0]], outs[1:]

    tiles = jnp.transpose(coupling, (1, 0, 2)).reshape(BLOCKS, 2, 8, DOF // 2, LANES)
    tiles = jnp.transpose(tiles, (0, 1, 3, 2, 4)).reshape(BLOCKS, 4 * LANES, LANES)
    halves = 2
    block = DOF // 2 // halves
    own_shape = jax.ShapeDtypeStruct((FACE_DEV, 2, DOF // 2, OWN_DEPTH), BF16)
    ghost_shape = jax.ShapeDtypeStruct((FACE_DEV, 2, DOF // 2, GHOST_DEPTH), BF16)
    place = lambda depth: pl.BlockSpec((8, 2, block, depth), lambda i: (i // halves, 0, i % halves, 0))
    own_high, own_low, ghost_high, ghost_low = pl.pallas_call(
        weights_kernel,
        grid=(2 * halves,),
        out_shape=[own_shape, own_shape, ghost_shape, ghost_shape],
        in_specs=[pl.BlockSpec((BLOCKS, 8 * block, LANES), lambda i: (0, i, 0))],
        out_specs=[place(OWN_DEPTH), place(OWN_DEPTH), place(GHOST_DEPTH), place(GHOST_DEPTH)],
        cost_estimate=pl.CostEstimate(flops=0, transcendentals=0, bytes_accessed=6 << 20),
        name="weights",
        **params(),
    )(tiles)

    own_call = pl.pallas_call(
        own_kernel,
        out_shape=field_shape,
        in_specs=[SMEM, VMEM, VMEM, VMEM],
        out_specs=VMEM,
        scratch_shapes=[pltpu.VMEM((ROWS, LANES), BF16)],
        cost_estimate=pl.CostEstimate(flops=1 << 30, transcendentals=0, bytes_accessed=3 << 20),
        name="own",
        **params(),
    )
    scratch = [pltpu.VMEM((4 * GHOST * DOF, LANES), F32), pltpu.VMEM((4 * GHOST * DOF, LANES), BF16)]
    ghost_call = pl.pallas_call(
        ghost_kernel,
        out_shape=[field_shape] + [send] * 4,
        in_specs=[SMEM, SMEM] + [VMEM] * 7,
        out_specs=[VMEM] * 5,
        scratch_shapes=scratch,
        name="ghost",
        **params(),
    )
    last_call = pl.pallas_call(
        last_kernel,
        out_shape=[shape_of(SYSTEM, LANES), shape_of(ROWS, 2 * LANES, BF16)],
        in_specs=[SMEM] + [VMEM] * 10,
        out_specs=[VMEM] * 2,
        scratch_shapes=[pltpu.VMEM((ROWS, LANES), F32)] + scratch,
        name="last",
        **params(),
    )
    for power in range(POWERS):
        received = exchange(sends)
        own_sum = own_call(face_columns, fields[-1], own_high, own_low)
        if power < POWERS - 1:
            outs = ghost_call(face_columns, ghost_lists, *received, own_sum, ghost_high, ghost_low)
            fields.append(outs[0])
            sends = outs[1:]
        else:
            system, basis = last_call(face_columns, *received, own_sum, ghost_high, ghost_low, *fields)
    mine, other = add_over_devices(system)
    result = shape_of(FACE_DEV, DOF * NRHS)
    return tuple(
        pl.pallas_call(
            finish_kernel,
            out_shape=[result, result],
            in_specs=[VMEM] * 3,
            out_specs=[VMEM] * 2,
            scratch_shapes=[pltpu.VMEM((2, ROWS, LANES), F32)],
            name="finish",
            **params(),
        )(mine, other, basis)
    )


def solution(mesh):
    placed = (
        P(("fx", "fy"), None),
        P(("fx", "fy"), None, None),
        P(("fx", "fy"), None),
        P(("fx", "fy"), None),
    )
    return jax.shard_map(
        on_device,
        mesh=mesh,
        in_specs=placed,
        out_specs=(P(("fx", "fy"), None), P(("fx", "fy"), None)),
        check_vma=False,
    )
```

time: 416 us -> 80.5 us (0.19)
  waiting for transfers between devices: 251 us -> 16.9 us
  matrix products: 42.2 us -> 0 us
  local copies, waits for them, and re-layouts: 41.9 us -> 3.4 us
  other arithmetic: 29.4 us -> 0.05 us
  Pallas kernels: 0 us -> 22.1 us
  between operations: 14.5 us -> 0.8 us
    psum x1 -> x0, waiting for transfers between devices: 248 us -> none  [on_device(): gram_total = lax.psum(local_gram, ('fx', 'fy'))]
    dot_general x10 -> x0, matrix products: 41.7 us -> none  [the longest x3 36.3 us: contract(): jnp.einsum('fkab,fkbr->far', block_mats, shaped, precision=lax.Precision....]
    pallas_call x0 -> x9, Pallas kernels: none -> 22.1 us  [the longest x1 9.86 us: on_device(): pl.pallas_call(finish_kernel, out_shape=[result, result], in_specs=[VMEM]...]
    reshape x9 -> x0, local copies, waits for them, and re-layouts: 22 us -> none  [the longest x3 13.9 us: contract(): shaped = picked.reshape(face_count, picked.shape[1], DOF, NRHS)]
    gather x18 -> x0, local copies, waits for them, and re-layouts: 18.8 us -> none  [the longest x6 8.28 us: on_device(): jnp.take(extended, face_columns, axis=0)]
    another operation x5 -> x0, other arithmetic: 17.5 us -> none  [the longest x3 9.45 us: solve_small(): factor = jnp.linalg.cholesky(normal_matrix)]
    ppermute x12 -> x23, waiting for transfers between devices: 2.55 us -> 16.9 us  [the longest x11 15.2 us: from_partner(): lax.ppermute(part, axis, [(i, i ^ distance) for i in range(lax.axis_size(...]
    select_n x16 -> x0, other arithmetic: 9.86 us -> none  [the longest x4 8.94 us: on_device(): jnp.take(extended, face_columns, axis=0)]
  transfers between devices with their start and end apart: 13 -> 23, of which waited for: 3 -> 11; matrix products, arithmetic and copies ran while one was open for 3% -> 0% of each run, Pallas kernels for 0% -> 8%
where the time goes in v1:
time: 80.5 us; the launch traced here: 80.2 us
  starting transfers between devices  37 us (46%)
  Pallas kernels  22.1 us (27%)
  waiting for transfers between devices  16.9 us (21%)
  local copies, waits for them, and re-layouts  3.4 us (4%)
    ppermute x12, starting transfers between devices, exchange(): lax.ppermute(send, axis, pairs_of(lax.axis_size(axis), second))  19.7 us
    ppermute x11, starting transfers between devices, from_partner(): lax.ppermute(part, axis, [(i, i ^ distance) for i in range(lax.axis_size(...  17.2 us
    ppermute x11, waiting for transfers between devices, from_partner(): lax.ppermute(part, axis, [(i, i ^ distance) for i in range(lax.axis_size(...  15.2 us
    pallas_call x1, Pallas kernels, on_device(): pl.pallas_call(finish_kernel, out_shape=[result, result], in_specs=[VMEM]...  9.86 us
    pallas_call x3, Pallas kernels, on_device(): own_sum = own_call(face_columns, fields[-1], own_high, own_low)  4.64 us
    unnamed x10, local copies, waits for them, and re-layouts  3.4 us
    pallas_call x2, Pallas kernels, on_device(): ghost_call(face_columns, ghost_lists, *received, own_sum, ghost_high, gho...  2.96 us
    pallas_call x1, Pallas kernels, on_device(): last_call(face_columns, *received, own_sum, ghost_high, ghost_low, *fields)  1.89 us
  transfers between devices with their start and end apart: 23, of which 11 were waited for; matrix products, arithmetic and copies ran while one was open for 0% of the time, Pallas kernels for 8%

profile of v1, /device:TPU:8, one launch (start us, length us, event | category | flops | bytes accessed | tf_op | source)
XLA Modules:
  0.0 80.2 jit_solution(1939687163273417440)
XLA Ops:
  3.2 1.6 %collective-permute-start = (f32[64,128]{1,0:T(8,128)S(1)}, f32[64,128]{1,0:T(8,128)S(1)}, u32[]{:S(2)}, u32[]{:S(2)}) collective-permute-start(f32[64,128]{1,0:T(8,128)S(1)} %get-tuple-element.23), channel_id=1, source_target_pairs={{0,8},{8,0},{16,24},{24,16},{32,40},{40,32},{48,56},{56,48},{64,72... | collective-permute-start | bytes 98312 | tf_op jit(solution)/shard_map/ppermute | solution.py:222
  4.8 7.4 %collective-permute-start.1 = (f32[64,128]{1,0:T(8,128)S(1)}, f32[64,128]{1,0:T(8,128)S(1)}, u32[]{:S(2)}, u32[]{:S(2)}) collective-permute-start(f32[64,128]{1,0:T(8,128)S(1)} %get-tuple-element.24), channel_id=1, source_target_pairs={{8,16},{24,32},{40,48},{56,64},{72,80},{88,96},{104,112},{120,128}... | collective-permute-start | bytes 98312 | tf_op jit(solution)/shard_map/ppermute | solution.py:222
  12.7 1.8 %copy-done = f32[16,11,4096]{2,0,1:T(8,128)S(1)} copy-done((f32[16,11,4096]{2,0,1:T(8,128)S(1)}, f32[16,11,4096]{2,0,1:T(8,128)}, u32[]{:S(2)}) %copy-start) | copy-done | bytes 2883608
  14.5 1.7 %weights.1 = (bf16[16,2,32,512]{3,2,1,0:T(8,128)(2,1)S(1)}, bf16[16,2,32,512]{3,2,1,0:T(8,128)(2,1)S(1)}, bf16[16,2,32,256]{3,2,1,0:T(8,128)(2,1)S(1)}, bf16[16,2,32,256]{3,2,1,0:T(8,128)(2,1)S(1)}) custom-call(f32[11,512,128]{2,1,0:T(8,128)S(1)} %bitcast.7), custom_call_target="tpu_custom_call" | custom-call | bytes 6291456 | tf_op jit(solution)/shard_map/weights/pallas_call | solution.py:268
  16.3 1.6 %own.3.sum_ref = f32[1024,128]{1,0:T(8,128)S(1)} custom-call(s32[16,11]{1,0:T(8,128)S(1)} %copy-done.2, f32[1024,128]{1,0:T(8,128)S(1)} %get-tuple-element.27.field_ref.f0, bf16[16,2,32,512]{3,2,1,0:T(8,128)(2,1)S(1)} %get-tuple-element.28.high_ref, bf16[16,2,32,512]{3,2,1,0:T(8,128)(2,1)S(1)} %get-tuple-element.29.low_ref), custom_call_target="tpu_custom_call" | custom-call | flops 1073741824 | bytes 3145728 | tf_op jit(solution)/shard_map/own/pallas_call | solution.py:310
  17.9 1.5 %ghost.2 = (f32[1024,128]{1,0:T(8,128)S(1)}, f32[64,128]{1,0:T(8,128)S(1)}, f32[64,128]{1,0:T(8,128)S(1)}, f32[64,128]{1,0:T(8,128)S(1)}, f32[64,128]{1,0:T(8,128)S(1)}) custom-call(s32[16,11]{1,0:T(8,128)S(1)} %copy-done.2, s32[4,4]{1,0:T(4,128)S(1)} %copy-done.4, f32[64,128]{1,0:T(8,128)S(1)} %collective-permute-done.r0, ...), custom_call_target="tpu_custom_call" | custom-call | tf_op jit(solution)/shard_map/ghost/pallas_call | solution.py:312
  19.5 1.6 %collective-permute-start.5 = (f32[64,128]{1,0:T(8,128)S(1)}, f32[64,128]{1,0:T(8,128)S(1)}, u32[]{:S(2)}, u32[]{:S(2)}) collective-permute-start(f32[64,128]{1,0:T(8,128)S(1)} %get-tuple-element.33), channel_id=1, source_target_pairs={{8,16},{24,32},{40,48},{56,64},{72,80},{88,96},{104,112},{120,128}... | collective-permute-start | bytes 98312 | tf_op jit(solution)/shard_map/ppermute | solution.py:222
  21.3 2.6 %collective-permute-start.7 = (f32[64,128]{1,0:T(8,128)S(1)}, f32[64,128]{1,0:T(8,128)S(1)}, u32[]{:S(2)}, u32[]{:S(2)}) collective-permute-start(f32[64,128]{1,0:T(8,128)S(1)} %get-tuple-element.35), channel_id=1, source_target_pairs={{1,2},{3,4},{5,6},{7,0},{2,1},{4,3},{6,5},{0,7},{9,10},{11,12},{13... | collective-permute-start | bytes 98312 | tf_op jit(solution)/shard_map/ppermute | solution.py:222
  23.8 1.5 %own.4.sum_ref = f32[1024,128]{1,0:T(8,128)S(1)} custom-call(s32[16,11]{1,0:T(8,128)S(1)} %copy-done.2, f32[1024,128]{1,0:T(8,128)S(1)} %get-tuple-element.36.field_ref.f1, bf16[16,2,32,512]{3,2,1,0:T(8,128)(2,1)S(1)} %get-tuple-element.28.high_ref, bf16[16,2,32,512]{3,2,1,0:T(8,128)(2,1)S(1)} %get-tuple-element.29.low_ref), custom_call_target="tpu_custom_call" | custom-call | flops 1073741824 | bytes 3145728 | tf_op jit(solution)/shard_map/own/pallas_call | solution.py:310
  25.4 1.6 %collective-permute-done.5.r1 = f32[64,128]{1,0:T(8,128)S(1)} collective-permute-done((f32[64,128]{1,0:T(8,128)S(1)}, f32[64,128]{1,0:T(8,128)S(1)}, u32[]{:S(2)}, u32[]{:S(2)}) %collective-permute-start.5) | collective-permute-done | bytes 32800 | tf_op jit(solution)/shard_map/ppermute | solution.py:222
  28.6 2.7 %collective-permute-start.9 = (f32[64,128]{1,0:T(8,128)S(1)}, f32[64,128]{1,0:T(8,128)S(1)}, u32[]{:S(2)}, u32[]{:S(2)}) collective-permute-start(f32[64,128]{1,0:T(8,128)S(1)} %get-tuple-element.38), channel_id=1, source_target_pairs={{8,16},{24,32},{40,48},{56,64},{72,80},{88,96},{104,112},{120,128}... | collective-permute-start | bytes 98312 | tf_op jit(solution)/shard_map/ppermute | solution.py:222
  31.4 3.0 %collective-permute-start.11 = (f32[64,128]{1,0:T(8,128)S(1)}, f32[64,128]{1,0:T(8,128)S(1)}, u32[]{:S(2)}, u32[]{:S(2)}) collective-permute-start(f32[64,128]{1,0:T(8,128)S(1)} %get-tuple-element.40), channel_id=1, source_target_pairs={{1,2},{3,4},{5,6},{7,0},{2,1},{4,3},{6,5},{0,7},{9,10},{11,12},{13... | collective-permute-start | bytes 98312 | tf_op jit(solution)/shard_map/ppermute | solution.py:222
  34.3 1.5 %own.5.sum_ref = f32[1024,128]{1,0:T(8,128)S(1)} custom-call(s32[16,11]{1,0:T(8,128)S(1)} %copy-done.2, f32[1024,128]{1,0:T(8,128)S(1)} %get-tuple-element.41.field_ref.f2, bf16[16,2,32,512]{3,2,1,0:T(8,128)(2,1)S(1)} %get-tuple-element.28.high_ref, bf16[16,2,32,512]{3,2,1,0:T(8,128)(2,1)S(1)} %get-tuple-element.29.low_ref), custom_call_target="tpu_custom_call" | custom-call | flops 1073741824 | bytes 3145728 | tf_op jit(solution)/shard_map/own/pallas_call | solution.py:310
  35.9 1.9 %last.1 = (f32[96,128]{1,0:T(8,128)S(1)}, bf16[1024,256]{1,0:T(8,128)(2,1)S(1)}) custom-call(s32[16,11]{1,0:T(8,128)S(1)} %copy-done.2, f32[64,128]{1,0:T(8,128)S(1)} %collective-permute-done.8.r0, f32[64,128]{1,0:T(8,128)S(1)} %collective-permute-done.9.r1, f32[64,128]{1,0:T(8,128)S(1)} %collective-permute-done.10.r2, ...), custom_call_target="tpu_custom_call" | custom-call | tf_op jit(solution)/shard_map/last/pallas_call | solution.py:316
  39.2 1.7 %collective-permute-start.15 = (f32[96,128]{1,0:T(8,128)S(1)}, f32[96,128]{1,0:T(8,128)S(1)}, u32[]{:S(2)}, u32[]{:S(2)}) collective-permute-start(f32[96,128]{1,0:T(8,128)S(1)} %add.30), channel_id=1, source_target_pairs={{0,6},{1,7},{2,4},{3,5},{4,2},{5,3},{6,0},{7,1},{8,14},{9,15},{10,... | collective-permute-start | bytes 147464 | tf_op jit(solution)/shard_map/ppermute | solution.py:232
  40.9 3.3 %collective-permute-start.14 = (f32[96,128]{1,0:T(8,128)S(1)}, f32[96,128]{1,0:T(8,128)S(1)}, u32[]{:S(2)}, u32[]{:S(2)}) collective-permute-start(f32[96,128]{1,0:T(8,128)S(1)} %add.30), channel_id=1, source_target_pairs={{0,4},{1,5},{2,6},{3,7},{4,0},{5,1},{6,2},{7,3},{8,12},{9,13},{10,... | collective-permute-start | bytes 147464 | tf_op jit(solution)/shard_map/ppermute | solution.py:232
  44.1 2.8 %collective-permute-done.14 = f32[96,128]{1,0:T(8,128)S(1)} collective-permute-done((f32[96,128]{1,0:T(8,128)S(1)}, f32[96,128]{1,0:T(8,128)S(1)}, u32[]{:S(2)}, u32[]{:S(2)}) %collective-permute-start.14) | collective-permute-done | bytes 49184 | tf_op jit(solution)/shard_map/ppermute | solution.py:232
  49.7 2.7 %collective-permute-start.16 = (f32[96,128]{1,0:T(8,128)S(1)}, f32[96,128]{1,0:T(8,128)S(1)}, u32[]{:S(2)}, u32[]{:S(2)}) collective-permute-start(f32[96,128]{1,0:T(8,128)S(1)} %add_add_fusion.2), channel_id=1, source_target_pairs={{0,8},{8,0},{16,24},{24,16},{32,40},{40,32},{48,56},{56,48},{64,72... | collective-permute-start | bytes 147464 | tf_op jit(solution)/shard_map/ppermute | solution.py:232
  55.0 2.0 %collective-permute-start.21 = (f32[96,128]{1,0:T(8,128)S(1)}, f32[96,128]{1,0:T(8,128)S(1)}, u32[]{:S(2)}, u32[]{:S(2)}) collective-permute-start(f32[96,128]{1,0:T(8,128)S(1)} %add_add_fusion.1), channel_id=1, source_target_pairs={{0,96},{8,104},{16,112},{24,120},{32,64},{40,72},{48,80},{56,88},{... | collective-permute-start | bytes 147464 | tf_op jit(solution)/shard_map/ppermute | solution.py:232
  57.1 2.4 %collective-permute-start.19 = (f32[96,128]{1,0:T(8,128)S(1)}, f32[96,128]{1,0:T(8,128)S(1)}, u32[]{:S(2)}, u32[]{:S(2)}) collective-permute-start(f32[96,128]{1,0:T(8,128)S(1)} %add_add_fusion.1), channel_id=1, source_target_pairs={{0,32},{8,40},{16,48},{24,56},{32,0},{40,8},{48,16},{56,24},{64,96... | collective-permute-start | bytes 147464 | tf_op jit(solution)/shard_map/ppermute | solution.py:232
  59.5 1.5 %collective-permute-done.21 = f32[96,128]{1,0:T(8,128)S(1)} collective-permute-done((f32[96,128]{1,0:T(8,128)S(1)}, f32[96,128]{1,0:T(8,128)S(1)}, u32[]{:S(2)}, u32[]{:S(2)}) %collective-permute-start.21) | collective-permute-done | bytes 49184 | tf_op jit(solution)/shard_map/ppermute | solution.py:232
  62.1 3.5 %collective-permute-start.22 = (f32[96,128]{1,0:T(8,128)S(1)}, f32[96,128]{1,0:T(8,128)S(1)}, u32[]{:S(2)}, u32[]{:S(2)}) collective-permute-start(f32[96,128]{1,0:T(8,128)S(1)} %add_add_fusion.mine), channel_id=1, source_target_pairs={{0,128},{8,136},{16,144},{24,152},{32,160},{40,168},{48,176},{56,1... | collective-permute-start | bytes 147464 | tf_op jit(solution)/shard_map/ppermute | solution.py:232
  65.6 4.7 %collective-permute-done.22.other = f32[96,128]{1,0:T(8,128)S(1)} collective-permute-done((f32[96,128]{1,0:T(8,128)S(1)}, f32[96,128]{1,0:T(8,128)S(1)}, u32[]{:S(2)}, u32[]{:S(2)}) %collective-permute-start.22) | collective-permute-done | bytes 49184 | tf_op jit(solution)/shard_map/ppermute | solution.py:232
  70.3 9.9 %finish.1 = (f32[16,2048]{1,0:T(8,128)}, f32[16,2048]{1,0:T(8,128)}) custom-call(f32[96,128]{1,0:T(8,128)S(1)} %add_add_fusion.mine, f32[96,128]{1,0:T(8,128)S(1)} %collective-permute-done.22.other, bf16[1024,256]{1,0:T(8,128)(2,1)S(1)} %get-tuple-element.43.basis_ref), custom_call_target="tpu_custom_call" | custom-call | tf_op jit(solution)/shard_map/finish/pallas_call | solution.py:320
  (45 shorter events, 12.9 us)
Async XLA Ops:
  2.2 14.1 %copy-start.2 = (s32[16,11]{1,0:T(8,128)S(1)}, s32[16,11]{1,0:T(8,128)}, u32[]{:S(2)}) copy-start(s32[16,11]{1,0:T(8,128)} %columns.11) | copy-start | bytes 2116
  3.2 14.7 %collective-permute-start = (f32[64,128]{1,0:T(8,128)S(1)}, f32[64,128]{1,0:T(8,128)S(1)}, u32[]{:S(2)}, u32[]{:S(2)}) collective-permute-start(f32[64,128]{1,0:T(8,128)S(1)} %get-tuple-element.23), channel_id=1, source_target_pairs={{0,8},{8,0},{16,24},{24,16},{32,40},{40,32},{48,56},{56,48},{64,72... | collective-permute-start | bytes 98312 | tf_op jit(solution)/shard_map/ppermute | solution.py:222
  4.8 13.1 %collective-permute-start.1 = (f32[64,128]{1,0:T(8,128)S(1)}, f32[64,128]{1,0:T(8,128)S(1)}, u32[]{:S(2)}, u32[]{:S(2)}) collective-permute-start(f32[64,128]{1,0:T(8,128)S(1)} %get-tuple-element.24), channel_id=1, source_target_pairs={{8,16},{24,32},{40,48},{56,64},{72,80},{88,96},{104,112},{120,128}... | collective-permute-start | bytes 98312 | tf_op jit(solution)/shard_map/ppermute | solution.py:222
  12.2 5.7 %collective-permute-start.2 = (f32[64,128]{1,0:T(8,128)S(1)}, f32[64,128]{1,0:T(8,128)S(1)}, u32[]{:S(2)}, u32[]{:S(2)}) collective-permute-start(f32[64,128]{1,0:T(8,128)S(1)} %get-tuple-element.25), channel_id=1, source_target_pairs={{0,1},{1,0},{2,3},{3,2},{4,5},{5,4},{6,7},{7,6},{8,9},{9,8},{10,11... | collective-permute-start | bytes 98312 | tf_op jit(solution)/shard_map/ppermute | solution.py:222
  12.2 5.7 %collective-permute-start.3 = (f32[64,128]{1,0:T(8,128)S(1)}, f32[64,128]{1,0:T(8,128)S(1)}, u32[]{:S(2)}, u32[]{:S(2)}) collective-permute-start(f32[64,128]{1,0:T(8,128)S(1)} %get-tuple-element.26), channel_id=1, source_target_pairs={{1,2},{3,4},{5,6},{7,0},{2,1},{4,3},{6,5},{0,7},{9,10},{11,12},{13... | collective-permute-start | bytes 98312 | tf_op jit(solution)/shard_map/ppermute | solution.py:222
  19.4 6.0 %collective-permute-start.4 = (f32[64,128]{1,0:T(8,128)S(1)}, f32[64,128]{1,0:T(8,128)S(1)}, u32[]{:S(2)}, u32[]{:S(2)}) collective-permute-start(f32[64,128]{1,0:T(8,128)S(1)} %get-tuple-element.32), channel_id=1, source_target_pairs={{0,8},{8,0},{16,24},{24,16},{32,40},{40,32},{48,56},{56,48},{64,72... | collective-permute-start | bytes 98312 | tf_op jit(solution)/shard_map/ppermute | solution.py:222
  19.5 7.5 %collective-permute-start.5 = (f32[64,128]{1,0:T(8,128)S(1)}, f32[64,128]{1,0:T(8,128)S(1)}, u32[]{:S(2)}, u32[]{:S(2)}) collective-permute-start(f32[64,128]{1,0:T(8,128)S(1)} %get-tuple-element.33), channel_id=1, source_target_pairs={{8,16},{24,32},{40,48},{56,64},{72,80},{88,96},{104,112},{120,128}... | collective-permute-start | bytes 98312 | tf_op jit(solution)/shard_map/ppermute | solution.py:222
  21.1 5.9 %collective-permute-start.6 = (f32[64,128]{1,0:T(8,128)S(1)}, f32[64,128]{1,0:T(8,128)S(1)}, u32[]{:S(2)}, u32[]{:S(2)}) collective-permute-start(f32[64,128]{1,0:T(8,128)S(1)} %get-tuple-element.34), channel_id=1, source_target_pairs={{0,1},{1,0},{2,3},{3,2},{4,5},{5,4},{6,7},{7,6},{8,9},{9,8},{10,11... | collective-permute-start | bytes 98312 | tf_op jit(solution)/shard_map/ppermute | solution.py:222
  21.3 5.8 %collective-permute-start.7 = (f32[64,128]{1,0:T(8,128)S(1)}, f32[64,128]{1,0:T(8,128)S(1)}, u32[]{:S(2)}, u32[]{:S(2)}) collective-permute-start(f32[64,128]{1,0:T(8,128)S(1)} %get-tuple-element.35), channel_id=1, source_target_pairs={{1,2},{3,4},{5,6},{7,0},{2,1},{4,3},{6,5},{0,7},{9,10},{11,12},{13... | collective-permute-start | bytes 98312 | tf_op jit(solution)/shard_map/ppermute | solution.py:222
  28.5 7.4 %collective-permute-start.8 = (f32[64,128]{1,0:T(8,128)S(1)}, f32[64,128]{1,0:T(8,128)S(1)}, u32[]{:S(2)}, u32[]{:S(2)}) collective-permute-start(f32[64,128]{1,0:T(8,128)S(1)} %get-tuple-element.37), channel_id=1, source_target_pairs={{0,8},{8,0},{16,24},{24,16},{32,40},{40,32},{48,56},{56,48},{64,72... | collective-permute-start | bytes 98312 | tf_op jit(solution)/shard_map/ppermute | solution.py:222
  28.6 7.3 %collective-permute-start.9 = (f32[64,128]{1,0:T(8,128)S(1)}, f32[64,128]{1,0:T(8,128)S(1)}, u32[]{:S(2)}, u32[]{:S(2)}) collective-permute-start(f32[64,128]{1,0:T(8,128)S(1)} %get-tuple-element.38), channel_id=1, source_target_pairs={{8,16},{24,32},{40,48},{56,64},{72,80},{88,96},{104,112},{120,128}... | collective-permute-start | bytes 98312 | tf_op jit(solution)/shard_map/ppermute | solution.py:222
  31.4 4.6 %collective-permute-start.10 = (f32[64,128]{1,0:T(8,128)S(1)}, f32[64,128]{1,0:T(8,128)S(1)}, u32[]{:S(2)}, u32[]{:S(2)}) collective-permute-start(f32[64,128]{1,0:T(8,128)S(1)} %get-tuple-element.39), channel_id=1, source_target_pairs={{0,1},{1,0},{2,3},{3,2},{4,5},{5,4},{6,7},{7,6},{8,9},{9,8},{10,11... | collective-permute-start | bytes 98312 | tf_op jit(solution)/shard_map/ppermute | solution.py:222
  31.4 4.6 %collective-permute-start.11 = (f32[64,128]{1,0:T(8,128)S(1)}, f32[64,128]{1,0:T(8,128)S(1)}, u32[]{:S(2)}, u32[]{:S(2)}) collective-permute-start(f32[64,128]{1,0:T(8,128)S(1)} %get-tuple-element.40), channel_id=1, source_target_pairs={{1,2},{3,4},{5,6},{7,0},{2,1},{4,3},{6,5},{0,7},{9,10},{11,12},{13... | collective-permute-start | bytes 98312 | tf_op jit(solution)/shard_map/ppermute | solution.py:222
  37.8 1.3 %collective-permute-start.12 = (f32[96,128]{1,0:T(8,128)S(1)}, f32[96,128]{1,0:T(8,128)S(1)}, u32[]{:S(2)}, u32[]{:S(2)}) collective-permute-start(f32[96,128]{1,0:T(8,128)S(1)} %get-tuple-element.42), channel_id=1, source_target_pairs={{0,1},{1,0},{2,3},{3,2},{4,5},{5,4},{6,7},{7,6},{8,9},{9,8},{10,11... | collective-permute-start | bytes 147464 | tf_op jit(solution)/shard_map/ppermute | solution.py:232
  39.2 5.0 %collective-permute-start.15 = (f32[96,128]{1,0:T(8,128)S(1)}, f32[96,128]{1,0:T(8,128)S(1)}, u32[]{:S(2)}, u32[]{:S(2)}) collective-permute-start(f32[96,128]{1,0:T(8,128)S(1)} %add.30), channel_id=1, source_target_pairs={{0,6},{1,7},{2,4},{3,5},{4,2},{5,3},{6,0},{7,1},{8,14},{9,15},{10,... | collective-permute-start | bytes 147464 | tf_op jit(solution)/shard_map/ppermute | solution.py:232
  40.9 6.1 %collective-permute-start.14 = (f32[96,128]{1,0:T(8,128)S(1)}, f32[96,128]{1,0:T(8,128)S(1)}, u32[]{:S(2)}, u32[]{:S(2)}) collective-permute-start(f32[96,128]{1,0:T(8,128)S(1)} %add.30), channel_id=1, source_target_pairs={{0,4},{1,5},{2,6},{3,7},{4,0},{5,1},{6,2},{7,3},{8,12},{9,13},{10,... | collective-permute-start | bytes 147464 | tf_op jit(solution)/shard_map/ppermute | solution.py:232
  44.1 4.1 %collective-permute-start.13 = (f32[96,128]{1,0:T(8,128)S(1)}, f32[96,128]{1,0:T(8,128)S(1)}, u32[]{:S(2)}, u32[]{:S(2)}) collective-permute-start(f32[96,128]{1,0:T(8,128)S(1)} %add.30), channel_id=1, source_target_pairs={{0,2},{1,3},{2,0},{3,1},{4,6},{5,7},{6,4},{7,5},{8,10},{9,11},{10,... | collective-permute-start | bytes 147464 | tf_op jit(solution)/shard_map/ppermute | solution.py:232
  48.2 5.4 %collective-permute-start.18 = (f32[96,128]{1,0:T(8,128)S(1)}, f32[96,128]{1,0:T(8,128)S(1)}, u32[]{:S(2)}, u32[]{:S(2)}) collective-permute-start(f32[96,128]{1,0:T(8,128)S(1)} %add_add_fusion.2), channel_id=1, source_target_pairs={{0,24},{8,16},{16,8},{24,0},{32,56},{40,48},{48,40},{56,32},{64,88... | collective-permute-start | bytes 147464 | tf_op jit(solution)/shard_map/ppermute | solution.py:232
  48.9 5.6 %collective-permute-start.17 = (f32[96,128]{1,0:T(8,128)S(1)}, f32[96,128]{1,0:T(8,128)S(1)}, u32[]{:S(2)}, u32[]{:S(2)}) collective-permute-start(f32[96,128]{1,0:T(8,128)S(1)} %add_add_fusion.2), channel_id=1, source_target_pairs={{0,16},{8,24},{16,0},{24,8},{32,48},{40,56},{48,32},{56,40},{64,80... | collective-permute-start | bytes 147464 | tf_op jit(solution)/shard_map/ppermute | solution.py:232
  49.7 5.3 %collective-permute-start.16 = (f32[96,128]{1,0:T(8,128)S(1)}, f32[96,128]{1,0:T(8,128)S(1)}, u32[]{:S(2)}, u32[]{:S(2)}) collective-permute-start(f32[96,128]{1,0:T(8,128)S(1)} %add_add_fusion.2), channel_id=1, source_target_pairs={{0,8},{8,0},{16,24},{24,16},{32,40},{40,32},{48,56},{56,48},{64,72... | collective-permute-start | bytes 147464 | tf_op jit(solution)/shard_map/ppermute | solution.py:232
  55.0 6.0 %collective-permute-start.21 = (f32[96,128]{1,0:T(8,128)S(1)}, f32[96,128]{1,0:T(8,128)S(1)}, u32[]{:S(2)}, u32[]{:S(2)}) collective-permute-start(f32[96,128]{1,0:T(8,128)S(1)} %add_add_fusion.1), channel_id=1, source_target_pairs={{0,96},{8,104},{16,112},{24,120},{32,64},{40,72},{48,80},{56,88},{... | collective-permute-start | bytes 147464 | tf_op jit(solution)/shard_map/ppermute | solution.py:232
  57.1 5.0 %collective-permute-start.20 = (f32[96,128]{1,0:T(8,128)S(1)}, f32[96,128]{1,0:T(8,128)S(1)}, u32[]{:S(2)}, u32[]{:S(2)}) collective-permute-start(f32[96,128]{1,0:T(8,128)S(1)} %add_add_fusion.1), channel_id=1, source_target_pairs={{0,64},{8,72},{16,80},{24,88},{32,96},{40,104},{48,112},{56,120},{... | collective-permute-start | bytes 147464 | tf_op jit(solution)/shard_map/ppermute | solution.py:232
  57.1 5.0 %collective-permute-start.19 = (f32[96,128]{1,0:T(8,128)S(1)}, f32[96,128]{1,0:T(8,128)S(1)}, u32[]{:S(2)}, u32[]{:S(2)}) collective-permute-start(f32[96,128]{1,0:T(8,128)S(1)} %add_add_fusion.1), channel_id=1, source_target_pairs={{0,32},{8,40},{16,48},{24,56},{32,0},{40,8},{48,16},{56,24},{64,96... | collective-permute-start | bytes 147464 | tf_op jit(solution)/shard_map/ppermute | solution.py:232
  62.1 8.2 %collective-permute-start.22 = (f32[96,128]{1,0:T(8,128)S(1)}, f32[96,128]{1,0:T(8,128)S(1)}, u32[]{:S(2)}, u32[]{:S(2)}) collective-permute-start(f32[96,128]{1,0:T(8,128)S(1)} %add_add_fusion.mine), channel_id=1, source_target_pairs={{0,128},{8,136},{16,144},{24,152},{32,160},{40,168},{48,176},{56,1... | collective-permute-start | bytes 147464 | tf_op jit(solution)/shard_map/ppermute | solution.py:232
  (4 other events, 6.8 us)

commit v2 on v1

v2 whole, which is shorter than its diff:
```python
import functools

import jax
import jax.numpy as jnp
from jax import lax
from jax.experimental import pallas as pl
from jax.experimental.pallas import tpu as pltpu
from jax.sharding import PartitionSpec as P

DOF = 64
NRHS = 32
BLOCKS = 11
OWNED = 7
POWERS = 3
FACE_DEV = 16
GHOST = 4
LANES = 128
COPIES = LANES // NRHS
ROWS = FACE_DEV * DOF
OWN_DEPTH = 512
GHOST_DEPTH = 256
SYSTEM = POWERS * NRHS
CHUNKS = 4
PIVOTS = 8

VMEM = pl.BlockSpec(memory_space=pltpu.VMEM)
ANY = pl.BlockSpec(memory_space=pl.ANY)
SMEM = pl.BlockSpec(memory_space=pltpu.SMEM)
HBM = pl.BlockSpec(memory_space=pltpu.HBM)
F32 = jnp.float32
BF16 = jnp.bfloat16


def shape_of(rows, columns, dtype=F32):
    return jax.ShapeDtypeStruct((rows, columns), dtype)


def lane_group(rows):
    return lax.broadcasted_iota(jnp.int32, (rows, LANES), 1) // NRHS


def by_group(group, parts):
    low = jnp.where(group == 0, parts[0], parts[1])
    high = jnp.where(group == 2, parts[2], parts[3])
    return jnp.where(group < 2, low, high)


def spread(tile):
    group = lane_group(tile.shape[0])
    turned = [tile] + [pltpu.roll(tile, NRHS * s, 1) for s in range(1, COPIES)]
    return [by_group(group, [turned[(c - j) % COPIES] for c in range(COPIES)]) for j in range(COPIES)]


def high_low(field):
    group = lane_group(field.shape[0])
    high = field.astype(BF16).astype(F32)
    return jnp.where(group % 2 == 0, high, field - high).astype(BF16)


def first_directions():
    odd_x = lax.rem(lax.axis_index("fx"), 2)
    odd_y = lax.rem(lax.axis_index("fy"), 2)
    return (odd_x, 1 - odd_x, 2 + odd_y, 3 - odd_y)


def inside(direction):
    fx, fy = lax.axis_index("fx"), lax.axis_index("fy")
    last_x, last_y = lax.axis_size("fx") - 1, lax.axis_size("fy") - 1
    out = (direction == 0) & (fx == 0) | (direction == 1) & (fx == last_x)
    return jnp.logical_not(out | (direction == 2) & (fy == 0) | (direction == 3) & (fy == last_y))


def write_sends(lists, field_ref, send_refs):
    group = lane_group(FACE_DEV)
    for direction, send_ref in zip(first_directions(), send_refs):
        for g in range(GHOST):
            start = lists[direction, g] * DOF
            parts = [field_ref[pl.ds(start + j, FACE_DEV, stride=COPIES), :] for j in range(COPIES)]
            send_ref[g * FACE_DEV : (g + 1) * FACE_DEV, :] = by_group(group, parts)


def first_kernel(lists_hbm, right_hbm, s0, s1, s2, s3, lists, right_ref, packed_ref, sems):
    copies = [
        pltpu.make_async_copy(lists_hbm, lists, sems.at[0]),
        pltpu.make_async_copy(right_hbm, right_ref, sems.at[1]),
    ]
    for copy in copies:
        copy.start()
    copies[1].wait()
    for t in range(DOF // COPIES):
        packed_ref[pl.ds(t, FACE_DEV, stride=FACE_DEV), :] = right_ref[:, t * LANES : (t + 1) * LANES]
    copies[0].wait()
    for direction, send_ref in zip(first_directions(), (s0, s1, s2, s3)):
        for g in range(GHOST):
            start = pl.multiple_of(lists[direction, g] * FACE_DEV, FACE_DEV)
            send_ref[g * FACE_DEV : (g + 1) * FACE_DEV, :] = packed_ref[pl.ds(start, FACE_DEV), :]


def weights_kernel(columns_any, lists_any, tiles_ref, right_ref, own_ref, ghost_ref, field_ref, columns, lists, sems):
    copies = [
        pltpu.make_async_copy(columns_any, columns, sems.at[0]),
        pltpu.make_async_copy(lists_any, lists, sems.at[1]),
    ]
    for copy in copies:
        copy.start()
    for t in range(DOF // COPIES):
        parts = spread(right_ref[:, t * LANES : (t + 1) * LANES])
        for j in range(COPIES):
            field_ref[pl.ds(COPIES * t + j, FACE_DEV, stride=DOF), :] = parts[j]
    rows = LANES // 8
    left = lax.broadcasted_iota(jnp.int32, (rows, LANES), 1) < DOF
    zero = jnp.zeros((rows, LANES), F32)
    order = list(range(OWNED)) + [None] + list(range(OWNED, BLOCKS))

    def chunk(i, carry):
        at = pl.ds(pl.multiple_of(lax.rem(i, 2) * rows, rows), rows)
        for face in range(8):
            tiles = [zero if k is None else tiles_ref[k, pl.ds(i * LANES + face, rows, stride=8), :] for k in order]
            turned = [zero if k is None else pltpu.roll(tile, DOF, 1) for k, tile in zip(order, tiles)]
            number = lax.div(i, 2) * 8 + face
            for q in range(len(order) // 2):
                even = jnp.where(left, tiles[2 * q], turned[2 * q + 1])
                odd = jnp.where(left, turned[2 * q], tiles[2 * q + 1])
                if q < OWN_DEPTH // LANES:
                    ref, lane = own_ref, q * LANES
                else:
                    ref, lane = ghost_ref, q * LANES - OWN_DEPTH
                for s, part in ((0, even), (1, odd)):
                    high = part.astype(BF16)
                    ref[number, s, at, lane : lane + LANES] = high
                    ref[number, 2 + s, at, lane : lane + LANES] = (part - high.astype(F32)).astype(BF16)
        return carry

    lax.fori_loop(0, CHUNKS, chunk, 0)
    for copy in copies:
        copy.wait()


def product(weights_ref, face, picked):
    weights = weights_ref[face].reshape(2 * DOF, picked.shape[0])
    both = jnp.dot(weights, picked, preferred_element_type=F32)
    both = both[:DOF] + both[DOF:]
    return both + pltpu.roll(both, NRHS, 1)


def pick(rows_ref, numbers):
    starts = [pl.multiple_of(number * DOF, DOF) for number in numbers]
    return jnp.concatenate([rows_ref[pl.ds(start, DOF), :] for start in starts], axis=0)


def own_kernel(columns, field_ref, weights_ref, sum_ref, split_ref):
    for face in range(FACE_DEV):
        at = slice(face * DOF, (face + 1) * DOF)
        split_ref[at, :] = high_low(field_ref[at, :])
    for face in range(FACE_DEV):
        numbers = [columns[face, k] for k in range(OWNED)]
        picked = pick(split_ref, numbers + numbers[:1])
        sum_ref[face * DOF : (face + 1) * DOF, :] = product(weights_ref, face, picked)


def add_ghosts(columns, received, sum_ref, weights_ref, field_ref, spread_ref, split_ref):
    for direction, received_ref in zip(first_directions(), received):
        keep = inside(direction)
        for g in range(GHOST):
            tile = received_ref[g * FACE_DEV : (g + 1) * FACE_DEV, :]
            parts = spread(jnp.where(keep, tile, 0.0))
            start = (direction * GHOST + g) * DOF
            for j in range(COPIES):
                spread_ref[pl.ds(start + j, FACE_DEV, stride=COPIES), :] = parts[j]
    for slot in range(4 * GHOST):
        at = slice(slot * DOF, (slot + 1) * DOF)
        split_ref[at, :] = high_low(spread_ref[at, :])
    for face in range(FACE_DEV):
        picked = pick(split_ref, [columns[face, k] - FACE_DEV for k in range(OWNED, BLOCKS)])
        total = sum_ref[face * DOF : (face + 1) * DOF, :] + product(weights_ref, face, picked)
        for s in range(2):
            rows = pl.ds(face * DOF + s, DOF // 2, stride=2)
            field_ref[rows, :] = total[s * DOF // 2 : (s + 1) * DOF // 2, :]


def ghost_kernel(columns, lists, r0, r1, r2, r3, sum_ref, weights_ref, field_ref, s0, s1, s2, s3, spread_ref, split_ref):
    add_ghosts(columns, (r0, r1, r2, r3), sum_ref, weights_ref, field_ref, spread_ref, split_ref)
    write_sends(lists, field_ref, (s0, s1, s2, s3))


def last_kernel(
    columns, r0, r1, r2, r3, sum_ref, weights_ref, f0, f1, f2, system_ref, basis_ref, f3, spread_ref, split_ref
):
    add_ghosts(columns, (r0, r1, r2, r3), sum_ref, weights_ref, f3, spread_ref, split_ref)
    group = lane_group(LANES)
    gram = jnp.zeros((LANES, 2 * LANES), F32)
    for part in range(ROWS // LANES):
        at = slice(part * LANES, (part + 1) * LANES)
        basis = by_group(group, [ref[at, :] for ref in (f0, f1, f2, f3)])
        high = basis.astype(BF16)
        low = (basis - high.astype(F32)).astype(BF16)
        both = jnp.concatenate([high, low], axis=1)
        basis_ref[at, :] = both
        gram = gram + lax.dot_general(high, both, (((0,), (0,)), ((), ())), preferred_element_type=F32)
    cross = gram[:, LANES:]
    full = gram[:, :LANES] + cross + cross.T
    pairs = full[:SYSTEM] + full[NRHS:]
    lane = lax.broadcasted_iota(jnp.int32, (SYSTEM, LANES), 1)
    system_ref[...] = pltpu.roll(pairs, SYSTEM, 1) + jnp.where(lane < SYSTEM, pairs, 0.0)


def eliminate(system):
    row = lax.broadcasted_iota(jnp.int32, (SYSTEM, LANES), 0)
    count = range(PIVOTS)
    for j in range(0, SYSTEM, PIVOTS):
        lines = [system[j + i : j + i + 1, :] for i in count]
        block = [[jnp.broadcast_to(lines[k][:, j + i : j + i + 1], (1, LANES)) for k in range(i + 1)] for i in count]
        inverse = [None] * PIVOTS
        lower = [[None] * PIVOTS for _ in count]
        for k in count:
            inverse[k] = 1.0 / block[k][k]
            for i in range(k + 1, PIVOTS):
                lower[i][k] = block[i][k] * inverse[k]
            for i in range(k + 1, PIVOTS):
                for q in range(k + 1, i + 1):
                    block[i][q] = block[i][q] - lower[i][k] * block[q][k]
        solved = list(lines)
        for k in count:
            for i in range(k + 1, PIVOTS):
                solved[i] = solved[i] - lower[i][k] * solved[k]
        solved = [solved[i] * inverse[i] for i in count]
        for k in reversed(count):
            for i in range(k):
                solved[i] = solved[i] - lower[k][i] * solved[k]
        factors = [system[:, j + i : j + i + 1] for i in count]
        for i in count:
            system = system - factors[i] * solved[i]
        for i in count:
            system = jnp.where(row == j + i, solved[i], system)
    return system


def finish_kernel(mine, other, basis_ref, solution_hbm, residual_hbm, out_ref, result_ref, sems):
    system = eliminate(mine[...] + other[...])
    lane = lax.broadcasted_iota(jnp.int32, (SYSTEM, LANES), 1)
    coeffs = jnp.where(lane >= SYSTEM, system, 0.0)
    coeffs = coeffs + pltpu.roll(coeffs, NRHS, 1)
    coeffs = coeffs + pltpu.roll(coeffs, 2 * NRHS, 1)
    zero = jnp.zeros((NRHS, LANES), F32)
    first_row = lax.broadcasted_iota(jnp.int32, (LANES, LANES), 0)
    first_lane = lax.broadcasted_iota(jnp.int32, (LANES, LANES), 1)
    first = jnp.where(first_row == first_lane % NRHS, 1.0, 0.0)
    padded = jnp.concatenate([coeffs, zero], axis=0)
    combo = first - (padded + jnp.concatenate([zero, coeffs], axis=0))
    both = jnp.concatenate([padded, combo], axis=1)
    high = both.astype(BF16)
    low = (both - high.astype(F32)).astype(BF16)
    twice = jnp.concatenate([high, high], axis=0)
    for part in range(ROWS // LANES):
        at = slice(part * LANES, (part + 1) * LANES)
        out = jnp.dot(basis_ref[at, :], twice, preferred_element_type=F32)
        out = out + jnp.dot(basis_ref[at, :LANES], low, preferred_element_type=F32)
        out_ref[0, at, :] = out[:, :LANES]
        out_ref[1, at, :] = out[:, LANES:]
    group = lane_group(FACE_DEV)
    copies = []
    for side, result_hbm in ((0, solution_hbm), (1, residual_hbm)):
        for t in range(DOF // COPIES):
            parts = [out_ref[side, pl.ds(COPIES * t + j, FACE_DEV, stride=DOF), :] for j in range(COPIES)]
            result_ref[side, :, t * LANES : (t + 1) * LANES] = by_group(group, parts)
        copies.append(pltpu.make_async_copy(result_ref.at[side], result_hbm, sems.at[side]))
        copies[side].start()
    for copy in copies:
        copy.wait()


def pairs_of(size, second):
    if not second:
        return [(i, i ^ 1) for i in range(size)]
    ahead = [(i, (i + 1) % size) for i in range(1, size, 2)]
    return ahead + [(b, a) for a, b in ahead]


def exchange(sends):
    routes = (("fx", True), ("fx", False), ("fy", True), ("fy", False))
    return [
        lax.ppermute(send, axis, pairs_of(lax.axis_size(axis), second))
        for send, (axis, second) in zip(sends, routes)
    ]


ROUNDS = (("fy", (1,)), ("fy", (2, 6, 4)), ("fx", (1, 3, 2)), ("fx", (4, 24, 28)))
LAST_ROUND = ("fx", 8)


def from_partner(part, axis, distance):
    return lax.ppermute(part, axis, [(i, i ^ distance) for i in range(lax.axis_size(axis))])


def add_over_devices(part):
    for axis, distances in ROUNDS:
        others = [from_partner(part, axis, d) for d in distances]
        part = part + others[0]
        if len(others) == 3:
            part = part + (others[1] + others[2])
    return part, from_partner(part, *LAST_ROUND)


def in_hbm(array):
    return pltpu.with_memory_space_constraint(array, pltpu.HBM)


def params():
    return dict(compiler_params=pltpu.CompilerParams(vmem_limit_bytes=32 << 20))


def on_device(right_side, coupling, face_columns, ghost_lists):
    send = shape_of(GHOST * FACE_DEV, LANES)
    field_shape = shape_of(ROWS, LANES)
    sends = pl.pallas_call(
        first_kernel,
        out_shape=[send] * 4,
        in_specs=[HBM, HBM],
        out_specs=[VMEM] * 4,
        scratch_shapes=[
            pltpu.SMEM((4, GHOST), jnp.int32),
            pltpu.VMEM((FACE_DEV, DOF * NRHS), F32),
            pltpu.VMEM((FACE_DEV * FACE_DEV, LANES), F32),
            pltpu.SemaphoreType.DMA((2,)),
        ],
        cost_estimate=pl.CostEstimate(flops=1 << 33, transcendentals=0, bytes_accessed=16 << 20),
        name="first",
        **params(),
    )(in_hbm(ghost_lists), in_hbm(right_side))

    tiles = jnp.transpose(coupling, (1, 0, 2)).reshape(BLOCKS, 2, 8, DOF // 2, LANES)
    tiles = jnp.transpose(tiles, (0, 1, 3, 2, 4)).reshape(BLOCKS, CHUNKS * LANES, LANES)
    own_weights, ghost_weights, field, columns, lists = pl.pallas_call(
        weights_kernel,
        out_shape=[
            jax.ShapeDtypeStruct((FACE_DEV, 4, DOF // 2, OWN_DEPTH), BF16),
            jax.ShapeDtypeStruct((FACE_DEV, 4, DOF // 2, GHOST_DEPTH), BF16),
            field_shape,
            pltpu.SMEM((FACE_DEV, BLOCKS), jnp.int32),
            pltpu.SMEM((4, GHOST), jnp.int32),
        ],
        in_specs=[ANY, ANY, VMEM, VMEM],
        out_specs=[VMEM] * 3 + [SMEM] * 2,
        scratch_shapes=[pltpu.SemaphoreType.DMA((2,))],
        cost_estimate=pl.CostEstimate(flops=0, transcendentals=0, bytes_accessed=6 << 20),
        name="weights",
        **params(),
    )(face_columns, ghost_lists, tiles, right_side)
    fields = [field]

    own_call = pl.pallas_call(
        own_kernel,
        out_shape=field_shape,
        in_specs=[SMEM, VMEM, VMEM],
        out_specs=VMEM,
        scratch_shapes=[pltpu.VMEM((ROWS, LANES), BF16)],
        cost_estimate=pl.CostEstimate(flops=1 << 30, transcendentals=0, bytes_accessed=3 << 20),
        name="own",
        **params(),
    )
    scratch = [
        pltpu.VMEM((4 * GHOST * DOF, LANES), F32),
        pltpu.VMEM((4 * GHOST * DOF, LANES), BF16),
    ]
    ghost_call = pl.pallas_call(
        ghost_kernel,
        out_shape=[field_shape] + [send] * 4,
        in_specs=[SMEM, SMEM] + [VMEM] * 6,
        out_specs=[VMEM] * 5,
        scratch_shapes=scratch,
        name="ghost",
        **params(),
    )
    last_call = pl.pallas_call(
        last_kernel,
        out_shape=[shape_of(SYSTEM, LANES), shape_of(ROWS, 2 * LANES, BF16)],
        in_specs=[SMEM] + [VMEM] * 9,
        out_specs=[VMEM] * 2,
        scratch_shapes=[pltpu.VMEM((ROWS, LANES), F32)] + scratch,
        name="last",
        **params(),
    )
    columns = pltpu.with_memory_space_constraint(columns, pltpu.SMEM)
    lists = pltpu.with_memory_space_constraint(lists, pltpu.SMEM)
    for power in range(POWERS):
        received = exchange(sends)
        own_sum = own_call(columns, fields[-1], own_weights)
        if power < POWERS - 1:
            outs = ghost_call(columns, lists, *received, own_sum, ghost_weights)
            fields.append(outs[0])
            sends = outs[1:]
        else:
            system, basis = last_call(columns, *received, own_sum, ghost_weights, *fields)
    mine, other = add_over_devices(system)
    result = shape_of(FACE_DEV, DOF * NRHS)
    return tuple(
        pl.pallas_call(
            finish_kernel,
            out_shape=[result, result],
            in_specs=[VMEM] * 3,
            out_specs=[HBM] * 2,
            scratch_shapes=[
                pltpu.VMEM((2, ROWS, LANES), F32),
                pltpu.VMEM((2, FACE_DEV, DOF * NRHS), F32),
                pltpu.SemaphoreType.DMA((2,)),
            ],
            name="finish",
            **params(),
        )(mine, other, basis)
    )


def solution(mesh):
    placed = (
        P(("fx", "fy"), None),
        P(("fx", "fy"), None, None),
        P(("fx", "fy"), None),
        P(("fx", "fy"), None),
    )
    return jax.shard_map(
        on_device,
        mesh=mesh,
        in_specs=placed,
        out_specs=(P(("fx", "fy"), None), P(("fx", "fy"), None)),
        check_vma=False,
    )
```

time: 80.5 us -> 66.9 us (0.83)
  Pallas kernels: 22.1 us -> 12.3 us
  local copies, waits for them, and re-layouts: 3.4 us -> 0.02 us
  starting transfers between devices: 37 us -> 33.9 us
  waiting for transfers between devices: 16.9 us -> 19.7 us
    pallas_call x1, Pallas kernels: 9.86 us -> 4.1 us  [on_device(): pl.pallas_call(finish_kernel, out_shape=[result, result], in_specs=[VMEM]...]
    pallas_call x8, Pallas kernels: 12.2 us -> 8.16 us  [the longest x3 2.6 us: on_device(): own_sum = own_call(columns, fields[-1], own_weights)]
    unnamed x10 -> x8, local copies, waits for them, and re-layouts: 3.4 us -> 0.02 us
    ppermute x11, starting transfers between devices: 17.2 us -> 14.2 us  [from_partner(): lax.ppermute(part, axis, [(i, i ^ distance) for i in range(lax.axis_size(...]
    ppermute x12, waiting for transfers between devices: 1.72 us -> 3.12 us  [exchange(): lax.ppermute(send, axis, pairs_of(lax.axis_size(axis), second))]
    ppermute x11, waiting for transfers between devices: 15.2 us -> 16.6 us  [from_partner(): lax.ppermute(part, axis, [(i, i ^ distance) for i in range(lax.axis_size(...]
  transfers between devices with their start and end apart: 23 -> 23, of which waited for: 11 -> 13; matrix products, arithmetic and copies ran while one was open for 0% -> 0% of each run, Pallas kernels for 8% -> 6%
where the time goes in v2:
time: 66.9 us; the launch traced here: 66.8 us
  starting transfers between devices  33.9 us (51%)
  waiting for transfers between devices  19.7 us (29%)
  Pallas kernels  12.3 us (18%)
  between operations  0.94 us (1%)
    ppermute x12, starting transfers between devices, exchange(): lax.ppermute(send, axis, pairs_of(lax.axis_size(axis), second))  19.6 us
    ppermute x11, waiting for transfers between devices, from_partner(): lax.ppermute(part, axis, [(i, i ^ distance) for i in range(lax.axis_size(...  16.6 us
    ppermute x11, starting transfers between devices, from_partner(): lax.ppermute(part, axis, [(i, i ^ distance) for i in range(lax.axis_size(...  14.2 us
    pallas_call x1, Pallas kernels, on_device(): pl.pallas_call(finish_kernel, out_shape=[result, result], in_specs=[VMEM]...  4.1 us
    ppermute x12, waiting for transfers between devices, exchange(): lax.ppermute(send, axis, pairs_of(lax.axis_size(axis), second))  3.12 us
    pallas_call x3, Pallas kernels, on_device(): own_sum = own_call(columns, fields[-1], own_weights)  2.6 us
    pallas_call x2, Pallas kernels, on_device(): outs = ghost_call(columns, lists, *received, own_sum, ghost_weights)  1.58 us
    pallas_call x1, Pallas kernels, on_device(): pl.pallas_call(weights_kernel, out_shape=[jax.ShapeDtypeStruct((FACE_DEV,...  1.5 us
  transfers between devices with their start and end apart: 23, of which 13 were waited for; matrix products, arithmetic and copies ran while one was open for 0% of the time, Pallas kernels for 6%

profile of v2, /device:TPU:8, one launch (start us, length us, event | category | flops | bytes accessed | tf_op | source)
XLA Modules:
  0.0 66.8 jit_solution(13422103678483576793)
XLA Ops:
  0.7 1.2 %first.1 = (f32[64,128]{1,0:T(8,128)S(1)}, f32[64,128]{1,0:T(8,128)S(1)}, f32[64,128]{1,0:T(8,128)S(1)}, f32[64,128]{1,0:T(8,128)S(1)}) custom-call(s32[4,4]{1,0:T(4,128)} %lists_hbm.1, f32[16,2048]{1,0:T(8,128)} %right_hbm.1), custom_call_target="tpu_custom_call" | custom-call | flops 8589934592 | bytes 16777216 | tf_op jit(solution)/shard_map/first/pallas_call | solution.py:315
  1.8 8.1 %collective-permute-start = (f32[64,128]{1,0:T(8,128)S(1)}, f32[64,128]{1,0:T(8,128)S(1)}, u32[]{:S(2)}, u32[]{:S(2)}) collective-permute-start(f32[64,128]{1,0:T(8,128)S(1)} %get-tuple-element.25), channel_id=1, source_target_pairs={{8,16},{24,32},{40,48},{56,64},{72,80},{88,96},{104,112},{120,128}... | collective-permute-start | bytes 98312 | tf_op jit(solution)/shard_map/ppermute | solution.py:282
  10.0 1.7 %collective-permute-start.3 = (f32[64,128]{1,0:T(8,128)S(1)}, f32[64,128]{1,0:T(8,128)S(1)}, u32[]{:S(2)}, u32[]{:S(2)}) collective-permute-start(f32[64,128]{1,0:T(8,128)S(1)} %get-tuple-element.28), channel_id=1, source_target_pairs={{0,1},{1,0},{2,3},{3,2},{4,5},{5,4},{6,7},{7,6},{8,9},{9,8},{10,11... | collective-permute-start | bytes 98312 | tf_op jit(solution)/shard_map/ppermute | solution.py:282
  11.7 1.5 %weights.1 = (bf16[16,4,32,512]{3,2,1,0:T(8,128)(2,1)S(1)}, bf16[16,4,32,256]{3,2,1,0:T(8,128)(2,1)S(1)}, f32[1024,128]{1,0:T(8,128)S(1)}, s32[16,11]{1,0:T(8,128)S(4)}, s32[4,4]{1,0:T(4,128)S(4)}) custom-call(s32[16,11]{1,0:T(8,128)S(1)} %copy-done.2, s32[4,4]{1,0:T(4,128)S(1)} %copy-done.3, f32[11,512,128]{2,1,0:T(8,128)S(1)} %bitcast.7, ...), custom_call_target="tpu_custom_call" | custom-call | bytes 6291456 | tf_op jit(solution)/shard_map/weights/pallas_call | solution.py:333
  14.9 3.2 %collective-permute-start.4 = (f32[64,128]{1,0:T(8,128)S(1)}, f32[64,128]{1,0:T(8,128)S(1)}, u32[]{:S(2)}, u32[]{:S(2)}) collective-permute-start(f32[64,128]{1,0:T(8,128)S(1)} %get-tuple-element.32), channel_id=1, source_target_pairs={{8,16},{24,32},{40,48},{56,64},{72,80},{88,96},{104,112},{120,128}... | collective-permute-start | bytes 98312 | tf_op jit(solution)/shard_map/ppermute | solution.py:282
  18.1 1.7 %collective-permute-start.7 = (f32[64,128]{1,0:T(8,128)S(1)}, f32[64,128]{1,0:T(8,128)S(1)}, u32[]{:S(2)}, u32[]{:S(2)}) collective-permute-start(f32[64,128]{1,0:T(8,128)S(1)} %get-tuple-element.35), channel_id=1, source_target_pairs={{0,1},{1,0},{2,3},{3,2},{4,5},{5,4},{6,7},{7,6},{8,9},{9,8},{10,11... | collective-permute-start | bytes 98312 | tf_op jit(solution)/shard_map/ppermute | solution.py:282
  20.7 1.5 %collective-permute-done.4.r0 = f32[64,128]{1,0:T(8,128)S(1)} collective-permute-done((f32[64,128]{1,0:T(8,128)S(1)}, f32[64,128]{1,0:T(8,128)S(1)}, u32[]{:S(2)}, u32[]{:S(2)}) %collective-permute-start.4) | collective-permute-done | bytes 32800 | tf_op jit(solution)/shard_map/ppermute | solution.py:282
  23.0 3.2 %collective-permute-start.8 = (f32[64,128]{1,0:T(8,128)S(1)}, f32[64,128]{1,0:T(8,128)S(1)}, u32[]{:S(2)}, u32[]{:S(2)}) collective-permute-start(f32[64,128]{1,0:T(8,128)S(1)} %get-tuple-element.37), channel_id=1, source_target_pairs={{8,16},{24,32},{40,48},{56,64},{72,80},{88,96},{104,112},{120,128}... | collective-permute-start | bytes 98312 | tf_op jit(solution)/shard_map/ppermute | solution.py:282
  26.2 1.7 %collective-permute-start.11 = (f32[64,128]{1,0:T(8,128)S(1)}, f32[64,128]{1,0:T(8,128)S(1)}, u32[]{:S(2)}, u32[]{:S(2)}) collective-permute-start(f32[64,128]{1,0:T(8,128)S(1)} %get-tuple-element.40), channel_id=1, source_target_pairs={{0,1},{1,0},{2,3},{3,2},{4,5},{5,4},{6,7},{7,6},{8,9},{9,8},{10,11... | collective-permute-start | bytes 98312 | tf_op jit(solution)/shard_map/ppermute | solution.py:282
  28.8 1.5 %collective-permute-done.8.r0 = f32[64,128]{1,0:T(8,128)S(1)} collective-permute-done((f32[64,128]{1,0:T(8,128)S(1)}, f32[64,128]{1,0:T(8,128)S(1)}, u32[]{:S(2)}, u32[]{:S(2)}) %collective-permute-start.8) | collective-permute-done | bytes 32800 | tf_op jit(solution)/shard_map/ppermute | solution.py:282
  30.4 1.3 %last.1 = (f32[96,128]{1,0:T(8,128)S(1)}, bf16[1024,256]{1,0:T(8,128)(2,1)S(1)}) custom-call(s32[16,11]{1,0:T(8,128)S(4)} %get-tuple-element.23.columns, f32[64,128]{1,0:T(8,128)S(1)} %collective-permute-done.8.r0, f32[64,128]{1,0:T(8,128)S(1)} %collective-permute-done.9.r1, f32[64,128]{1,0:T(8,128)S(1)} %collective-permute-done.10.r2, ...), custom_call_target="tpu_custom_call" | custom-call | tf_op jit(solution)/shard_map/last/pallas_call | solution.py:393
  31.8 1.2 %collective-permute-done.12 = f32[96,128]{1,0:T(8,128)S(1)} collective-permute-done((f32[96,128]{1,0:T(8,128)S(1)}, f32[96,128]{1,0:T(8,128)S(1)}, u32[]{:S(2)}, u32[]{:S(2)}) %collective-permute-start.12) | collective-permute-done | bytes 49184 | tf_op jit(solution)/shard_map/ppermute | solution.py:292
  33.0 2.2 %collective-permute-start.15 = (f32[96,128]{1,0:T(8,128)S(1)}, f32[96,128]{1,0:T(8,128)S(1)}, u32[]{:S(2)}, u32[]{:S(2)}) collective-permute-start(f32[96,128]{1,0:T(8,128)S(1)} %add.30), channel_id=1, source_target_pairs={{0,4},{1,5},{2,6},{3,7},{4,0},{5,1},{6,2},{7,3},{8,12},{9,13},{10,... | collective-permute-start | bytes 147464 | tf_op jit(solution)/shard_map/ppermute | solution.py:292
  35.5 2.3 %collective-permute-start.13 = (f32[96,128]{1,0:T(8,128)S(1)}, f32[96,128]{1,0:T(8,128)S(1)}, u32[]{:S(2)}, u32[]{:S(2)}) collective-permute-start(f32[96,128]{1,0:T(8,128)S(1)} %add.30), channel_id=1, source_target_pairs={{0,2},{1,3},{2,0},{3,1},{4,6},{5,7},{6,4},{7,5},{8,10},{9,11},{10,... | collective-permute-start | bytes 147464 | tf_op jit(solution)/shard_map/ppermute | solution.py:292
  37.8 1.0 %collective-permute-done.15 = f32[96,128]{1,0:T(8,128)S(1)} collective-permute-done((f32[96,128]{1,0:T(8,128)S(1)}, f32[96,128]{1,0:T(8,128)S(1)}, u32[]{:S(2)}, u32[]{:S(2)}) %collective-permute-start.15) | collective-permute-done | bytes 49184 | tf_op jit(solution)/shard_map/ppermute | solution.py:292
  39.9 1.1 %collective-permute-start.18 = (f32[96,128]{1,0:T(8,128)S(1)}, f32[96,128]{1,0:T(8,128)S(1)}, u32[]{:S(2)}, u32[]{:S(2)}) collective-permute-start(f32[96,128]{1,0:T(8,128)S(1)} %add_add_fusion.2), channel_id=1, source_target_pairs={{0,16},{8,24},{16,0},{24,8},{32,48},{40,56},{48,32},{56,40},{64,80... | collective-permute-start | bytes 147464 | tf_op jit(solution)/shard_map/ppermute | solution.py:292
  41.0 3.3 %collective-permute-start.17 = (f32[96,128]{1,0:T(8,128)S(1)}, f32[96,128]{1,0:T(8,128)S(1)}, u32[]{:S(2)}, u32[]{:S(2)}) collective-permute-start(f32[96,128]{1,0:T(8,128)S(1)} %add_add_fusion.2), channel_id=1, source_target_pairs={{0,24},{8,16},{16,8},{24,0},{32,56},{40,48},{48,40},{56,32},{64,88... | collective-permute-start | bytes 147464 | tf_op jit(solution)/shard_map/ppermute | solution.py:292
  44.3 1.6 %collective-permute-done.18 = f32[96,128]{1,0:T(8,128)S(1)} collective-permute-done((f32[96,128]{1,0:T(8,128)S(1)}, f32[96,128]{1,0:T(8,128)S(1)}, u32[]{:S(2)}, u32[]{:S(2)}) %collective-permute-start.18) | collective-permute-done | bytes 49184 | tf_op jit(solution)/shard_map/ppermute | solution.py:292
  46.4 2.0 %collective-permute-done.16 = f32[96,128]{1,0:T(8,128)S(1)} collective-permute-done((f32[96,128]{1,0:T(8,128)S(1)}, f32[96,128]{1,0:T(8,128)S(1)}, u32[]{:S(2)}, u32[]{:S(2)}) %collective-permute-start.16) | collective-permute-done | bytes 49184 | tf_op jit(solution)/shard_map/ppermute | solution.py:292
  48.4 1.3 %collective-permute-start.21 = (f32[96,128]{1,0:T(8,128)S(1)}, f32[96,128]{1,0:T(8,128)S(1)}, u32[]{:S(2)}, u32[]{:S(2)}) collective-permute-start(f32[96,128]{1,0:T(8,128)S(1)} %add_add_fusion.1), channel_id=1, source_target_pairs={{0,224},{8,232},{16,240},{24,248},{32,192},{40,200},{48,208},{56,2... | collective-permute-start | bytes 147464 | tf_op jit(solution)/shard_map/ppermute | solution.py:292
  49.8 3.0 %collective-permute-start.20 = (f32[96,128]{1,0:T(8,128)S(1)}, f32[96,128]{1,0:T(8,128)S(1)}, u32[]{:S(2)}, u32[]{:S(2)}) collective-permute-start(f32[96,128]{1,0:T(8,128)S(1)} %add_add_fusion.1), channel_id=1, source_target_pairs={{0,192},{8,200},{16,208},{24,216},{32,224},{40,232},{48,240},{56,2... | collective-permute-start | bytes 147464 | tf_op jit(solution)/shard_map/ppermute | solution.py:292
  53.8 2.2 %collective-permute-done.20 = f32[96,128]{1,0:T(8,128)S(1)} collective-permute-done((f32[96,128]{1,0:T(8,128)S(1)}, f32[96,128]{1,0:T(8,128)S(1)}, u32[]{:S(2)}, u32[]{:S(2)}) %collective-permute-start.20) | collective-permute-done | bytes 49184 | tf_op jit(solution)/shard_map/ppermute | solution.py:292
  57.1 5.5 %collective-permute-done.22.other = f32[96,128]{1,0:T(8,128)S(1)} collective-permute-done((f32[96,128]{1,0:T(8,128)S(1)}, f32[96,128]{1,0:T(8,128)S(1)}, u32[]{:S(2)}, u32[]{:S(2)}) %collective-permute-start.22) | collective-permute-done | bytes 49184 | tf_op jit(solution)/shard_map/ppermute | solution.py:292
  62.6 4.1 %finish.1 = (f32[16,2048]{1,0:T(8,128)}, f32[16,2048]{1,0:T(8,128)}) custom-call(f32[96,128]{1,0:T(8,128)S(1)} %add_add_fusion.mine, f32[96,128]{1,0:T(8,128)S(1)} %collective-permute-done.22.other, bf16[1024,256]{1,0:T(8,128)(2,1)S(1)} %get-tuple-element.43.basis_ref), custom_call_target="tpu_custom_call" | custom-call | tf_op jit(solution)/shard_map/finish/pallas_call | solution.py:397
  (43 shorter events, 8.4 us)
Async XLA Ops:
  0.6 11.0 %copy-start.3 = (s32[4,4]{1,0:T(4,128)S(1)}, s32[4,4]{1,0:T(4,128)}, u32[]{:S(2)}) copy-start(s32[4,4]{1,0:T(4,128)} %lists_hbm.1) | copy-start | bytes 196
  1.8 12.2 %collective-permute-start = (f32[64,128]{1,0:T(8,128)S(1)}, f32[64,128]{1,0:T(8,128)S(1)}, u32[]{:S(2)}, u32[]{:S(2)}) collective-permute-start(f32[64,128]{1,0:T(8,128)S(1)} %get-tuple-element.25), channel_id=1, source_target_pairs={{8,16},{24,32},{40,48},{56,64},{72,80},{88,96},{104,112},{120,128}... | collective-permute-start | bytes 98312 | tf_op jit(solution)/shard_map/ppermute | solution.py:282
  10.0 4.1 %collective-permute-start.1 = (f32[64,128]{1,0:T(8,128)S(1)}, f32[64,128]{1,0:T(8,128)S(1)}, u32[]{:S(2)}, u32[]{:S(2)}) collective-permute-start(f32[64,128]{1,0:T(8,128)S(1)} %get-tuple-element.26), channel_id=1, source_target_pairs={{0,8},{8,0},{16,24},{24,16},{32,40},{40,32},{48,56},{56,48},{64,72... | collective-permute-start | bytes 98312 | tf_op jit(solution)/shard_map/ppermute | solution.py:282
  10.0 4.1 %collective-permute-start.2 = (f32[64,128]{1,0:T(8,128)S(1)}, f32[64,128]{1,0:T(8,128)S(1)}, u32[]{:S(2)}, u32[]{:S(2)}) collective-permute-start(f32[64,128]{1,0:T(8,128)S(1)} %get-tuple-element.27), channel_id=1, source_target_pairs={{1,2},{3,4},{5,6},{7,0},{2,1},{4,3},{6,5},{0,7},{9,10},{11,12},{13... | collective-permute-start | bytes 98312 | tf_op jit(solution)/shard_map/ppermute | solution.py:282
  10.0 4.1 %collective-permute-start.3 = (f32[64,128]{1,0:T(8,128)S(1)}, f32[64,128]{1,0:T(8,128)S(1)}, u32[]{:S(2)}, u32[]{:S(2)}) collective-permute-start(f32[64,128]{1,0:T(8,128)S(1)} %get-tuple-element.28), channel_id=1, source_target_pairs={{0,1},{1,0},{2,3},{3,2},{4,5},{5,4},{6,7},{7,6},{8,9},{9,8},{10,11... | collective-permute-start | bytes 98312 | tf_op jit(solution)/shard_map/ppermute | solution.py:282
  14.9 7.3 %collective-permute-start.4 = (f32[64,128]{1,0:T(8,128)S(1)}, f32[64,128]{1,0:T(8,128)S(1)}, u32[]{:S(2)}, u32[]{:S(2)}) collective-permute-start(f32[64,128]{1,0:T(8,128)S(1)} %get-tuple-element.32), channel_id=1, source_target_pairs={{8,16},{24,32},{40,48},{56,64},{72,80},{88,96},{104,112},{120,128}... | collective-permute-start | bytes 98312 | tf_op jit(solution)/shard_map/ppermute | solution.py:282
  18.1 4.1 %collective-permute-start.5 = (f32[64,128]{1,0:T(8,128)S(1)}, f32[64,128]{1,0:T(8,128)S(1)}, u32[]{:S(2)}, u32[]{:S(2)}) collective-permute-start(f32[64,128]{1,0:T(8,128)S(1)} %get-tuple-element.33), channel_id=1, source_target_pairs={{0,8},{8,0},{16,24},{24,16},{32,40},{40,32},{48,56},{56,48},{64,72... | collective-permute-start | bytes 98312 | tf_op jit(solution)/shard_map/ppermute | solution.py:282
  18.1 4.1 %collective-permute-start.6 = (f32[64,128]{1,0:T(8,128)S(1)}, f32[64,128]{1,0:T(8,128)S(1)}, u32[]{:S(2)}, u32[]{:S(2)}) collective-permute-start(f32[64,128]{1,0:T(8,128)S(1)} %get-tuple-element.34), channel_id=1, source_target_pairs={{1,2},{3,4},{5,6},{7,0},{2,1},{4,3},{6,5},{0,7},{9,10},{11,12},{13... | collective-permute-start | bytes 98312 | tf_op jit(solution)/shard_map/ppermute | solution.py:282
  18.1 4.1 %collective-permute-start.7 = (f32[64,128]{1,0:T(8,128)S(1)}, f32[64,128]{1,0:T(8,128)S(1)}, u32[]{:S(2)}, u32[]{:S(2)}) collective-permute-start(f32[64,128]{1,0:T(8,128)S(1)} %get-tuple-element.35), channel_id=1, source_target_pairs={{0,1},{1,0},{2,3},{3,2},{4,5},{5,4},{6,7},{7,6},{8,9},{9,8},{10,11... | collective-permute-start | bytes 98312 | tf_op jit(solution)/shard_map/ppermute | solution.py:282
  23.0 7.3 %collective-permute-start.8 = (f32[64,128]{1,0:T(8,128)S(1)}, f32[64,128]{1,0:T(8,128)S(1)}, u32[]{:S(2)}, u32[]{:S(2)}) collective-permute-start(f32[64,128]{1,0:T(8,128)S(1)} %get-tuple-element.37), channel_id=1, source_target_pairs={{8,16},{24,32},{40,48},{56,64},{72,80},{88,96},{104,112},{120,128}... | collective-permute-start | bytes 98312 | tf_op jit(solution)/shard_map/ppermute | solution.py:282
  26.2 4.1 %collective-permute-start.9 = (f32[64,128]{1,0:T(8,128)S(1)}, f32[64,128]{1,0:T(8,128)S(1)}, u32[]{:S(2)}, u32[]{:S(2)}) collective-permute-start(f32[64,128]{1,0:T(8,128)S(1)} %get-tuple-element.38), channel_id=1, source_target_pairs={{0,8},{8,0},{16,24},{24,16},{32,40},{40,32},{48,56},{56,48},{64,72... | collective-permute-start | bytes 98312 | tf_op jit(solution)/shard_map/ppermute | solution.py:282
  26.2 4.1 %collective-permute-start.10 = (f32[64,128]{1,0:T(8,128)S(1)}, f32[64,128]{1,0:T(8,128)S(1)}, u32[]{:S(2)}, u32[]{:S(2)}) collective-permute-start(f32[64,128]{1,0:T(8,128)S(1)} %get-tuple-element.39), channel_id=1, source_target_pairs={{1,2},{3,4},{5,6},{7,0},{2,1},{4,3},{6,5},{0,7},{9,10},{11,12},{13... | collective-permute-start | bytes 98312 | tf_op jit(solution)/shard_map/ppermute | solution.py:282
  26.2 4.1 %collective-permute-start.11 = (f32[64,128]{1,0:T(8,128)S(1)}, f32[64,128]{1,0:T(8,128)S(1)}, u32[]{:S(2)}, u32[]{:S(2)}) collective-permute-start(f32[64,128]{1,0:T(8,128)S(1)} %get-tuple-element.40), channel_id=1, source_target_pairs={{0,1},{1,0},{2,3},{3,2},{4,5},{5,4},{6,7},{7,6},{8,9},{9,8},{10,11... | collective-permute-start | bytes 98312 | tf_op jit(solution)/shard_map/ppermute | solution.py:282
  31.7 1.3 %collective-permute-start.12 = (f32[96,128]{1,0:T(8,128)S(1)}, f32[96,128]{1,0:T(8,128)S(1)}, u32[]{:S(2)}, u32[]{:S(2)}) collective-permute-start(f32[96,128]{1,0:T(8,128)S(1)} %get-tuple-element.42), channel_id=1, source_target_pairs={{0,1},{1,0},{2,3},{3,2},{4,5},{5,4},{6,7},{7,6},{8,9},{9,8},{10,11... | collective-permute-start | bytes 147464 | tf_op jit(solution)/shard_map/ppermute | solution.py:292
  33.0 5.7 %collective-permute-start.15 = (f32[96,128]{1,0:T(8,128)S(1)}, f32[96,128]{1,0:T(8,128)S(1)}, u32[]{:S(2)}, u32[]{:S(2)}) collective-permute-start(f32[96,128]{1,0:T(8,128)S(1)} %add.30), channel_id=1, source_target_pairs={{0,4},{1,5},{2,6},{3,7},{4,0},{5,1},{6,2},{7,3},{8,12},{9,13},{10,... | collective-permute-start | bytes 147464 | tf_op jit(solution)/shard_map/ppermute | solution.py:292
  35.2 4.2 %collective-permute-start.14 = (f32[96,128]{1,0:T(8,128)S(1)}, f32[96,128]{1,0:T(8,128)S(1)}, u32[]{:S(2)}, u32[]{:S(2)}) collective-permute-start(f32[96,128]{1,0:T(8,128)S(1)} %add.30), channel_id=1, source_target_pairs={{0,6},{1,7},{2,4},{3,5},{4,2},{5,3},{6,0},{7,1},{8,14},{9,15},{10,... | collective-permute-start | bytes 147464 | tf_op jit(solution)/shard_map/ppermute | solution.py:292
  35.5 4.3 %collective-permute-start.13 = (f32[96,128]{1,0:T(8,128)S(1)}, f32[96,128]{1,0:T(8,128)S(1)}, u32[]{:S(2)}, u32[]{:S(2)}) collective-permute-start(f32[96,128]{1,0:T(8,128)S(1)} %add.30), channel_id=1, source_target_pairs={{0,2},{1,3},{2,0},{3,1},{4,6},{5,7},{6,4},{7,5},{8,10},{9,11},{10,... | collective-permute-start | bytes 147464 | tf_op jit(solution)/shard_map/ppermute | solution.py:292
  39.9 6.0 %collective-permute-start.18 = (f32[96,128]{1,0:T(8,128)S(1)}, f32[96,128]{1,0:T(8,128)S(1)}, u32[]{:S(2)}, u32[]{:S(2)}) collective-permute-start(f32[96,128]{1,0:T(8,128)S(1)} %add_add_fusion.2), channel_id=1, source_target_pairs={{0,16},{8,24},{16,0},{24,8},{32,48},{40,56},{48,32},{56,40},{64,80... | collective-permute-start | bytes 147464 | tf_op jit(solution)/shard_map/ppermute | solution.py:292
  41.0 5.4 %collective-permute-start.17 = (f32[96,128]{1,0:T(8,128)S(1)}, f32[96,128]{1,0:T(8,128)S(1)}, u32[]{:S(2)}, u32[]{:S(2)}) collective-permute-start(f32[96,128]{1,0:T(8,128)S(1)} %add_add_fusion.2), channel_id=1, source_target_pairs={{0,24},{8,16},{16,8},{24,0},{32,56},{40,48},{48,40},{56,32},{64,88... | collective-permute-start | bytes 147464 | tf_op jit(solution)/shard_map/ppermute | solution.py:292
  44.3 4.1 %collective-permute-start.16 = (f32[96,128]{1,0:T(8,128)S(1)}, f32[96,128]{1,0:T(8,128)S(1)}, u32[]{:S(2)}, u32[]{:S(2)}) collective-permute-start(f32[96,128]{1,0:T(8,128)S(1)} %add_add_fusion.2), channel_id=1, source_target_pairs={{0,8},{8,0},{16,24},{24,16},{32,40},{40,32},{48,56},{56,48},{64,72... | collective-permute-start | bytes 147464 | tf_op jit(solution)/shard_map/ppermute | solution.py:292
  48.4 5.4 %collective-permute-start.21 = (f32[96,128]{1,0:T(8,128)S(1)}, f32[96,128]{1,0:T(8,128)S(1)}, u32[]{:S(2)}, u32[]{:S(2)}) collective-permute-start(f32[96,128]{1,0:T(8,128)S(1)} %add_add_fusion.1), channel_id=1, source_target_pairs={{0,224},{8,232},{16,240},{24,248},{32,192},{40,200},{48,208},{56,2... | collective-permute-start | bytes 147464 | tf_op jit(solution)/shard_map/ppermute | solution.py:292
  49.8 6.3 %collective-permute-start.20 = (f32[96,128]{1,0:T(8,128)S(1)}, f32[96,128]{1,0:T(8,128)S(1)}, u32[]{:S(2)}, u32[]{:S(2)}) collective-permute-start(f32[96,128]{1,0:T(8,128)S(1)} %add_add_fusion.1), channel_id=1, source_target_pairs={{0,192},{8,200},{16,208},{24,216},{32,224},{40,232},{48,240},{56,2... | collective-permute-start | bytes 147464 | tf_op jit(solution)/shard_map/ppermute | solution.py:292
  52.8 4.2 %collective-permute-start.19 = (f32[96,128]{1,0:T(8,128)S(1)}, f32[96,128]{1,0:T(8,128)S(1)}, u32[]{:S(2)}, u32[]{:S(2)}) collective-permute-start(f32[96,128]{1,0:T(8,128)S(1)} %add_add_fusion.1), channel_id=1, source_target_pairs={{0,32},{8,40},{16,48},{24,56},{32,0},{40,8},{48,16},{56,24},{64,96... | collective-permute-start | bytes 147464 | tf_op jit(solution)/shard_map/ppermute | solution.py:292
  57.0 5.6 %collective-permute-start.22 = (f32[96,128]{1,0:T(8,128)S(1)}, f32[96,128]{1,0:T(8,128)S(1)}, u32[]{:S(2)}, u32[]{:S(2)}) collective-permute-start(f32[96,128]{1,0:T(8,128)S(1)} %add_add_fusion.mine), channel_id=1, source_target_pairs={{0,64},{8,72},{16,80},{24,88},{32,96},{40,104},{48,112},{56,120},{... | collective-permute-start | bytes 147464 | tf_op jit(solution)/shard_map/ppermute | solution.py:292
  (3 other events, 33.1 us)

commit v3 on v2

--- a/solution.py
+++ b/solution.py
@@ -20,6 +20,7 @@
 OWN_DEPTH = 512
 GHOST_DEPTH = 256
 SYSTEM = POWERS * NRHS
+PACKED = 9 * NRHS * NRHS // LANES
 CHUNKS = 4
 PIVOTS = 8
 
@@ -60,7 +61,7 @@
 def first_directions():
     odd_x = lax.rem(lax.axis_index("fx"), 2)
     odd_y = lax.rem(lax.axis_index("fy"), 2)
-    return (odd_x, 1 - odd_x, 2 + odd_y, 3 - odd_y)
+    return (odd_x, 2 + odd_y, 1 - odd_x, 3 - odd_y)
 
 
 def inside(direction):
@@ -116,11 +117,12 @@
         at = pl.ds(pl.multiple_of(lax.rem(i, 2) * rows, rows), rows)
         for face in range(8):
             tiles = [zero if k is None else tiles_ref[k, pl.ds(i * LANES + face, rows, stride=8), :] for k in order]
-            turned = [zero if k is None else pltpu.roll(tile, DOF, 1) for k, tile in zip(order, tiles)]
             number = lax.div(i, 2) * 8 + face
             for q in range(len(order) // 2):
-                even = jnp.where(left, tiles[2 * q], turned[2 * q + 1])
-                odd = jnp.where(left, turned[2 * q], tiles[2 * q + 1])
+                one, two = tiles[2 * q : 2 * q + 2]
+                moved = pltpu.roll(jnp.where(left, two, one), DOF, 1)
+                even = jnp.where(left, one, moved)
+                odd = jnp.where(left, moved, two)
                 if q < OWN_DEPTH // LANES:
                     ref, lane = own_ref, q * LANES
                 else:
@@ -183,6 +185,25 @@
     write_sends(lists, field_ref, (s0, s1, s2, s3))
 
 
+def pack(system):
+    lane = lax.broadcasted_iota(jnp.int32, (NRHS, LANES), 1)
+    bottom = system[2 * NRHS :]
+    middle = jnp.where(lane < NRHS, pltpu.roll(bottom, 2 * NRHS, 1), system[NRHS : 2 * NRHS])
+    pieces = [pltpu.roll(bottom[8 * i : 8 * i + 8], NRHS * (i + 1) % LANES, 1) if i < 3 else bottom[24:] for i in range(4)]
+    return jnp.concatenate([system[:NRHS], middle, by_group(lane_group(8), pieces)], axis=0)
+
+
+def unpack(packed):
+    lane = lax.broadcasted_iota(jnp.int32, (NRHS, LANES), 1)
+    middle, tail = packed[NRHS : 2 * NRHS], packed[2 * NRHS :]
+    terms = [pltpu.roll(tail, NRHS * (3 - i), 1) if i < 3 else tail for i in range(4)]
+    bottom = jnp.where(lane < SYSTEM, pltpu.roll(middle, 2 * NRHS, 1), jnp.concatenate(terms, axis=0))
+    upper = jnp.concatenate([packed[: 2 * NRHS], bottom, jnp.zeros((NRHS, LANES), F32)], axis=0)
+    block_row = lax.broadcasted_iota(jnp.int32, (SYSTEM, LANES), 0) // NRHS
+    block_lane = lax.broadcasted_iota(jnp.int32, (SYSTEM, LANES), 1) // NRHS
+    return jnp.where(block_lane < block_row, upper.T[:SYSTEM], upper[:SYSTEM])
+
+
 def last_kernel(
     columns, r0, r1, r2, r3, sum_ref, weights_ref, f0, f1, f2, system_ref, basis_ref, f3, spread_ref, split_ref
 ):
@@ -201,7 +222,7 @@
     full = gram[:, :LANES] + cross + cross.T
     pairs = full[:SYSTEM] + full[NRHS:]
     lane = lax.broadcasted_iota(jnp.int32, (SYSTEM, LANES), 1)
-    system_ref[...] = pltpu.roll(pairs, SYSTEM, 1) + jnp.where(lane < SYSTEM, pairs, 0.0)
+    system_ref[...] = pack(pltpu.roll(pairs, SYSTEM, 1) + jnp.where(lane < SYSTEM, pairs, 0.0))
 
 
 def eliminate(system):
@@ -236,7 +257,7 @@
 
 
 def finish_kernel(mine, other, basis_ref, solution_hbm, residual_hbm, out_ref, result_ref, sems):
-    system = eliminate(mine[...] + other[...])
+    system = eliminate(unpack(mine[...] + other[...]))
     lane = lax.broadcasted_iota(jnp.int32, (SYSTEM, LANES), 1)
     coeffs = jnp.where(lane >= SYSTEM, system, 0.0)
     coeffs = coeffs + pltpu.roll(coeffs, NRHS, 1)
@@ -277,7 +298,7 @@
 
 
 def exchange(sends):
-    routes = (("fx", True), ("fx", False), ("fy", True), ("fy", False))
+    routes = (("fx", True), ("fy", True), ("fx", False), ("fy", False))
     return [
         lax.ppermute(send, axis, pairs_of(lax.axis_size(axis), second))
         for send, (axis, second) in zip(sends, routes)
@@ -373,7 +394,7 @@
     )
     last_call = pl.pallas_call(
         last_kernel,
-        out_shape=[shape_of(SYSTEM, LANES), shape_of(ROWS, 2 * LANES, BF16)],
+        out_shape=[shape_of(PACKED, LANES), shape_of(ROWS, 2 * LANES, BF16)],
         in_specs=[SMEM] + [VMEM] * 9,
         out_specs=[VMEM] * 2,
         scratch_shapes=[pltpu.VMEM((ROWS, LANES), F32)] + scratch,

time: 66.9 us -> 64.8 us (0.969)
  waiting for transfers between devices: 19.7 us -> 17 us
    ppermute x11, waiting for transfers between devices: 16.6 us -> 13.8 us  [from_partner(): lax.ppermute(part, axis, [(i, i ^ distance) for i in range(lax.axis_size(...]
where the time goes in v3:
time: 64.8 us; the launch traced here: 64.7 us
  starting transfers between devices  34.2 us (53%)
  waiting for transfers between devices  17 us (26%)
  Pallas kernels  12.5 us (19%)
  between operations  0.94 us (1%)
    ppermute x12, starting transfers between devices, exchange(): lax.ppermute(send, axis, pairs_of(lax.axis_size(axis), second))  19.6 us
    ppermute x11, starting transfers between devices, from_partner(): lax.ppermute(part, axis, [(i, i ^ distance) for i in range(lax.axis_size(...  14.6 us
    ppermute x11, waiting for transfers between devices, from_partner(): lax.ppermute(part, axis, [(i, i ^ distance) for i in range(lax.axis_size(...  13.8 us
    pallas_call x1, Pallas kernels, on_device(): pl.pallas_call(finish_kernel, out_shape=[result, result], in_specs=[VMEM]...  4.24 us
    ppermute x12, waiting for transfers between devices, exchange(): lax.ppermute(send, axis, pairs_of(lax.axis_size(axis), second))  3.19 us
    pallas_call x3, Pallas kernels, on_device(): own_sum = own_call(columns, fields[-1], own_weights)  2.6 us
    pallas_call x2, Pallas kernels, on_device(): outs = ghost_call(columns, lists, *received, own_sum, ghost_weights)  1.58 us
    pallas_call x1, Pallas kernels, on_device(): pl.pallas_call(weights_kernel, out_shape=[jax.ShapeDtypeStruct((FACE_DEV,...  1.53 us
  transfers between devices with their start and end apart: 23, of which 13 were waited for; matrix products, arithmetic and copies ran while one was open for 0% of the time, Pallas kernels for 6%

profile of v3, /device:TPU:8, one launch (start us, length us, event | category | flops | bytes accessed | tf_op | source)
XLA Modules:
  0.0 64.7 jit_solution(3118246845399286381)
XLA Ops:
  0.7 1.2 %first.1 = (f32[64,128]{1,0:T(8,128)S(1)}, f32[64,128]{1,0:T(8,128)S(1)}, f32[64,128]{1,0:T(8,128)S(1)}, f32[64,128]{1,0:T(8,128)S(1)}) custom-call(s32[4,4]{1,0:T(4,128)} %lists_hbm.1, f32[16,2048]{1,0:T(8,128)} %right_hbm.1), custom_call_target="tpu_custom_call" | custom-call | flops 8589934592 | bytes 16777216 | tf_op jit(solution)/shard_map/first/pallas_call | solution.py:336
  1.8 8.1 %collective-permute-start = (f32[64,128]{1,0:T(8,128)S(1)}, f32[64,128]{1,0:T(8,128)S(1)}, u32[]{:S(2)}, u32[]{:S(2)}) collective-permute-start(f32[64,128]{1,0:T(8,128)S(1)} %get-tuple-element.25), channel_id=1, source_target_pairs={{8,16},{24,32},{40,48},{56,64},{72,80},{88,96},{104,112},{120,128}... | collective-permute-start | bytes 98312 | tf_op jit(solution)/shard_map/ppermute | solution.py:303
  10.0 1.7 %collective-permute-start.3 = (f32[64,128]{1,0:T(8,128)S(1)}, f32[64,128]{1,0:T(8,128)S(1)}, u32[]{:S(2)}, u32[]{:S(2)}) collective-permute-start(f32[64,128]{1,0:T(8,128)S(1)} %get-tuple-element.28), channel_id=1, source_target_pairs={{0,1},{1,0},{2,3},{3,2},{4,5},{5,4},{6,7},{7,6},{8,9},{9,8},{10,11... | collective-permute-start | bytes 98312 | tf_op jit(solution)/shard_map/ppermute | solution.py:303
  11.7 1.5 %weights.1 = (bf16[16,4,32,512]{3,2,1,0:T(8,128)(2,1)S(1)}, bf16[16,4,32,256]{3,2,1,0:T(8,128)(2,1)S(1)}, f32[1024,128]{1,0:T(8,128)S(1)}, s32[16,11]{1,0:T(8,128)S(4)}, s32[4,4]{1,0:T(4,128)S(4)}) custom-call(s32[16,11]{1,0:T(8,128)S(1)} %copy-done.2, s32[4,4]{1,0:T(4,128)S(1)} %copy-done.3, f32[11,512,128]{2,1,0:T(8,128)S(1)} %bitcast.7, ...), custom_call_target="tpu_custom_call" | custom-call | bytes 6291456 | tf_op jit(solution)/shard_map/weights/pallas_call | solution.py:354
  14.9 3.2 %collective-permute-start.4 = (f32[64,128]{1,0:T(8,128)S(1)}, f32[64,128]{1,0:T(8,128)S(1)}, u32[]{:S(2)}, u32[]{:S(2)}) collective-permute-start(f32[64,128]{1,0:T(8,128)S(1)} %get-tuple-element.32), channel_id=1, source_target_pairs={{8,16},{24,32},{40,48},{56,64},{72,80},{88,96},{104,112},{120,128}... | collective-permute-start | bytes 98312 | tf_op jit(solution)/shard_map/ppermute | solution.py:303
  18.2 1.6 %collective-permute-start.7 = (f32[64,128]{1,0:T(8,128)S(1)}, f32[64,128]{1,0:T(8,128)S(1)}, u32[]{:S(2)}, u32[]{:S(2)}) collective-permute-start(f32[64,128]{1,0:T(8,128)S(1)} %get-tuple-element.35), channel_id=1, source_target_pairs={{0,1},{1,0},{2,3},{3,2},{4,5},{5,4},{6,7},{7,6},{8,9},{9,8},{10,11... | collective-permute-start | bytes 98312 | tf_op jit(solution)/shard_map/ppermute | solution.py:303
  20.7 1.6 %collective-permute-done.4.r0 = f32[64,128]{1,0:T(8,128)S(1)} collective-permute-done((f32[64,128]{1,0:T(8,128)S(1)}, f32[64,128]{1,0:T(8,128)S(1)}, u32[]{:S(2)}, u32[]{:S(2)}) %collective-permute-start.4) | collective-permute-done | bytes 32800 | tf_op jit(solution)/shard_map/ppermute | solution.py:303
  23.1 3.2 %collective-permute-start.8 = (f32[64,128]{1,0:T(8,128)S(1)}, f32[64,128]{1,0:T(8,128)S(1)}, u32[]{:S(2)}, u32[]{:S(2)}) collective-permute-start(f32[64,128]{1,0:T(8,128)S(1)} %get-tuple-element.37), channel_id=1, source_target_pairs={{8,16},{24,32},{40,48},{56,64},{72,80},{88,96},{104,112},{120,128}... | collective-permute-start | bytes 98312 | tf_op jit(solution)/shard_map/ppermute | solution.py:303
  26.2 1.7 %collective-permute-start.11 = (f32[64,128]{1,0:T(8,128)S(1)}, f32[64,128]{1,0:T(8,128)S(1)}, u32[]{:S(2)}, u32[]{:S(2)}) collective-permute-start(f32[64,128]{1,0:T(8,128)S(1)} %get-tuple-element.40), channel_id=1, source_target_pairs={{0,1},{1,0},{2,3},{3,2},{4,5},{5,4},{6,7},{7,6},{8,9},{9,8},{10,11... | collective-permute-start | bytes 98312 | tf_op jit(solution)/shard_map/ppermute | solution.py:303
  28.8 1.6 %collective-permute-done.8.r0 = f32[64,128]{1,0:T(8,128)S(1)} collective-permute-done((f32[64,128]{1,0:T(8,128)S(1)}, f32[64,128]{1,0:T(8,128)S(1)}, u32[]{:S(2)}, u32[]{:S(2)}) %collective-permute-start.8) | collective-permute-done | bytes 32800 | tf_op jit(solution)/shard_map/ppermute | solution.py:303
  30.4 1.4 %last.1 = (f32[72,128]{1,0:T(8,128)S(1)}, bf16[1024,256]{1,0:T(8,128)(2,1)S(1)}) custom-call(s32[16,11]{1,0:T(8,128)S(4)} %get-tuple-element.23.columns, f32[64,128]{1,0:T(8,128)S(1)} %collective-permute-done.8.r0, f32[64,128]{1,0:T(8,128)S(1)} %collective-permute-done.9.r1, f32[64,128]{1,0:T(8,128)S(1)} %collective-permute-done.10.r2, ...), custom_call_target="tpu_custom_call" | custom-call | tf_op jit(solution)/shard_map/last/pallas_call | solution.py:414
  32.2 0.9 %collective-permute-done.12 = f32[72,128]{1,0:T(8,128)S(1)} collective-permute-done((f32[72,128]{1,0:T(8,128)S(1)}, f32[72,128]{1,0:T(8,128)S(1)}, u32[]{:S(2)}, u32[]{:S(2)}) %collective-permute-start.12) | collective-permute-done | bytes 36896 | tf_op jit(solution)/shard_map/ppermute | solution.py:313
  33.1 2.3 %collective-permute-start.15 = (f32[72,128]{1,0:T(8,128)S(1)}, f32[72,128]{1,0:T(8,128)S(1)}, u32[]{:S(2)}, u32[]{:S(2)}) collective-permute-start(f32[72,128]{1,0:T(8,128)S(1)} %add.30), channel_id=1, source_target_pairs={{0,4},{1,5},{2,6},{3,7},{4,0},{5,1},{6,2},{7,3},{8,12},{9,13},{10,... | collective-permute-start | bytes 110600 | tf_op jit(solution)/shard_map/ppermute | solution.py:313
  35.4 1.7 %collective-permute-start.14 = (f32[72,128]{1,0:T(8,128)S(1)}, f32[72,128]{1,0:T(8,128)S(1)}, u32[]{:S(2)}, u32[]{:S(2)}) collective-permute-start(f32[72,128]{1,0:T(8,128)S(1)} %add.30), channel_id=1, source_target_pairs={{0,6},{1,7},{2,4},{3,5},{4,2},{5,3},{6,0},{7,1},{8,14},{9,15},{10,... | collective-permute-start | bytes 110600 | tf_op jit(solution)/shard_map/ppermute | solution.py:313
  39.4 1.7 %collective-permute-done.13 = f32[72,128]{1,0:T(8,128)S(1)} collective-permute-done((f32[72,128]{1,0:T(8,128)S(1)}, f32[72,128]{1,0:T(8,128)S(1)}, u32[]{:S(2)}, u32[]{:S(2)}) %collective-permute-start.13) | collective-permute-done | bytes 36896 | tf_op jit(solution)/shard_map/ppermute | solution.py:313
  41.2 2.7 %collective-permute-start.17 = (f32[72,128]{1,0:T(8,128)S(1)}, f32[72,128]{1,0:T(8,128)S(1)}, u32[]{:S(2)}, u32[]{:S(2)}) collective-permute-start(f32[72,128]{1,0:T(8,128)S(1)} %add_add_fusion.2), channel_id=1, source_target_pairs={{0,24},{8,16},{16,8},{24,0},{32,56},{40,48},{48,40},{56,32},{64,88... | collective-permute-start | bytes 110600 | tf_op jit(solution)/shard_map/ppermute | solution.py:313
  44.7 2.1 %collective-permute-done.18 = f32[72,128]{1,0:T(8,128)S(1)} collective-permute-done((f32[72,128]{1,0:T(8,128)S(1)}, f32[72,128]{1,0:T(8,128)S(1)}, u32[]{:S(2)}, u32[]{:S(2)}) %collective-permute-start.18) | collective-permute-done | bytes 36896 | tf_op jit(solution)/shard_map/ppermute | solution.py:313
  46.9 1.0 %collective-permute-done.16 = f32[72,128]{1,0:T(8,128)S(1)} collective-permute-done((f32[72,128]{1,0:T(8,128)S(1)}, f32[72,128]{1,0:T(8,128)S(1)}, u32[]{:S(2)}, u32[]{:S(2)}) %collective-permute-start.16) | collective-permute-done | bytes 36896 | tf_op jit(solution)/shard_map/ppermute | solution.py:313
  49.1 3.6 %collective-permute-start.19 = (f32[72,128]{1,0:T(8,128)S(1)}, f32[72,128]{1,0:T(8,128)S(1)}, u32[]{:S(2)}, u32[]{:S(2)}) collective-permute-start(f32[72,128]{1,0:T(8,128)S(1)} %add_add_fusion.1), channel_id=1, source_target_pairs={{0,32},{8,40},{16,48},{24,56},{32,0},{40,8},{48,16},{56,24},{64,96... | collective-permute-start | bytes 110600 | tf_op jit(solution)/shard_map/ppermute | solution.py:313
  53.1 1.4 %collective-permute-done.20 = f32[72,128]{1,0:T(8,128)S(1)} collective-permute-done((f32[72,128]{1,0:T(8,128)S(1)}, f32[72,128]{1,0:T(8,128)S(1)}, u32[]{:S(2)}, u32[]{:S(2)}) %collective-permute-start.20) | collective-permute-done | bytes 36896 | tf_op jit(solution)/shard_map/ppermute | solution.py:313
  54.5 0.9 %collective-permute-done.19 = f32[72,128]{1,0:T(8,128)S(1)} collective-permute-done((f32[72,128]{1,0:T(8,128)S(1)}, f32[72,128]{1,0:T(8,128)S(1)}, u32[]{:S(2)}, u32[]{:S(2)}) %collective-permute-start.19) | collective-permute-done | bytes 36896 | tf_op jit(solution)/shard_map/ppermute | solution.py:313
  55.4 1.2 %collective-permute-start.22 = (f32[72,128]{1,0:T(8,128)S(1)}, f32[72,128]{1,0:T(8,128)S(1)}, u32[]{:S(2)}, u32[]{:S(2)}) collective-permute-start(f32[72,128]{1,0:T(8,128)S(1)} %add_add_fusion.mine), channel_id=1, source_target_pairs={{0,64},{8,72},{16,80},{24,88},{32,96},{40,104},{48,112},{56,120},{... | collective-permute-start | bytes 110600 | tf_op jit(solution)/shard_map/ppermute | solution.py:313
  56.6 3.7 %collective-permute-done.22.other = f32[72,128]{1,0:T(8,128)S(1)} collective-permute-done((f32[72,128]{1,0:T(8,128)S(1)}, f32[72,128]{1,0:T(8,128)S(1)}, u32[]{:S(2)}, u32[]{:S(2)}) %collective-permute-start.22) | collective-permute-done | bytes 36896 | tf_op jit(solution)/shard_map/ppermute | solution.py:313
  60.4 4.2 %finish.1 = (f32[16,2048]{1,0:T(8,128)}, f32[16,2048]{1,0:T(8,128)}) custom-call(f32[72,128]{1,0:T(8,128)S(1)} %add_add_fusion.mine, f32[72,128]{1,0:T(8,128)S(1)} %collective-permute-done.22.other, bf16[1024,256]{1,0:T(8,128)(2,1)S(1)} %get-tuple-element.43.basis_ref), custom_call_target="tpu_custom_call" | custom-call | tf_op jit(solution)/shard_map/finish/pallas_call | solution.py:418
  (43 shorter events, 9.6 us)
Async XLA Ops:
  0.6 11.0 %copy-start.3 = (s32[4,4]{1,0:T(4,128)S(1)}, s32[4,4]{1,0:T(4,128)}, u32[]{:S(2)}) copy-start(s32[4,4]{1,0:T(4,128)} %lists_hbm.1) | copy-start | bytes 196
  1.8 12.3 %collective-permute-start = (f32[64,128]{1,0:T(8,128)S(1)}, f32[64,128]{1,0:T(8,128)S(1)}, u32[]{:S(2)}, u32[]{:S(2)}) collective-permute-start(f32[64,128]{1,0:T(8,128)S(1)} %get-tuple-element.25), channel_id=1, source_target_pairs={{8,16},{24,32},{40,48},{56,64},{72,80},{88,96},{104,112},{120,128}... | collective-permute-start | bytes 98312 | tf_op jit(solution)/shard_map/ppermute | solution.py:303
  10.0 4.1 %collective-permute-start.1 = (f32[64,128]{1,0:T(8,128)S(1)}, f32[64,128]{1,0:T(8,128)S(1)}, u32[]{:S(2)}, u32[]{:S(2)}) collective-permute-start(f32[64,128]{1,0:T(8,128)S(1)} %get-tuple-element.26), channel_id=1, source_target_pairs={{1,2},{3,4},{5,6},{7,0},{2,1},{4,3},{6,5},{0,7},{9,10},{11,12},{13... | collective-permute-start | bytes 98312 | tf_op jit(solution)/shard_map/ppermute | solution.py:303
  10.0 4.1 %collective-permute-start.2 = (f32[64,128]{1,0:T(8,128)S(1)}, f32[64,128]{1,0:T(8,128)S(1)}, u32[]{:S(2)}, u32[]{:S(2)}) collective-permute-start(f32[64,128]{1,0:T(8,128)S(1)} %get-tuple-element.27), channel_id=1, source_target_pairs={{0,8},{8,0},{16,24},{24,16},{32,40},{40,32},{48,56},{56,48},{64,72... | collective-permute-start | bytes 98312 | tf_op jit(solution)/shard_map/ppermute | solution.py:303
  10.0 4.1 %collective-permute-start.3 = (f32[64,128]{1,0:T(8,128)S(1)}, f32[64,128]{1,0:T(8,128)S(1)}, u32[]{:S(2)}, u32[]{:S(2)}) collective-permute-start(f32[64,128]{1,0:T(8,128)S(1)} %get-tuple-element.28), channel_id=1, source_target_pairs={{0,1},{1,0},{2,3},{3,2},{4,5},{5,4},{6,7},{7,6},{8,9},{9,8},{10,11... | collective-permute-start | bytes 98312 | tf_op jit(solution)/shard_map/ppermute | solution.py:303
  14.9 7.3 %collective-permute-start.4 = (f32[64,128]{1,0:T(8,128)S(1)}, f32[64,128]{1,0:T(8,128)S(1)}, u32[]{:S(2)}, u32[]{:S(2)}) collective-permute-start(f32[64,128]{1,0:T(8,128)S(1)} %get-tuple-element.32), channel_id=1, source_target_pairs={{8,16},{24,32},{40,48},{56,64},{72,80},{88,96},{104,112},{120,128}... | collective-permute-start | bytes 98312 | tf_op jit(solution)/shard_map/ppermute | solution.py:303
  18.1 4.2 %collective-permute-start.5 = (f32[64,128]{1,0:T(8,128)S(1)}, f32[64,128]{1,0:T(8,128)S(1)}, u32[]{:S(2)}, u32[]{:S(2)}) collective-permute-start(f32[64,128]{1,0:T(8,128)S(1)} %get-tuple-element.33), channel_id=1, source_target_pairs={{1,2},{3,4},{5,6},{7,0},{2,1},{4,3},{6,5},{0,7},{9,10},{11,12},{13... | collective-permute-start | bytes 98312 | tf_op jit(solution)/shard_map/ppermute | solution.py:303
  18.1 4.2 %collective-permute-start.6 = (f32[64,128]{1,0:T(8,128)S(1)}, f32[64,128]{1,0:T(8,128)S(1)}, u32[]{:S(2)}, u32[]{:S(2)}) collective-permute-start(f32[64,128]{1,0:T(8,128)S(1)} %get-tuple-element.34), channel_id=1, source_target_pairs={{0,8},{8,0},{16,24},{24,16},{32,40},{40,32},{48,56},{56,48},{64,72... | collective-permute-start | bytes 98312 | tf_op jit(solution)/shard_map/ppermute | solution.py:303
  18.2 4.1 %collective-permute-start.7 = (f32[64,128]{1,0:T(8,128)S(1)}, f32[64,128]{1,0:T(8,128)S(1)}, u32[]{:S(2)}, u32[]{:S(2)}) collective-permute-start(f32[64,128]{1,0:T(8,128)S(1)} %get-tuple-element.35), channel_id=1, source_target_pairs={{0,1},{1,0},{2,3},{3,2},{4,5},{5,4},{6,7},{7,6},{8,9},{9,8},{10,11... | collective-permute-start | bytes 98312 | tf_op jit(solution)/shard_map/ppermute | solution.py:303
  23.1 7.3 %collective-permute-start.8 = (f32[64,128]{1,0:T(8,128)S(1)}, f32[64,128]{1,0:T(8,128)S(1)}, u32[]{:S(2)}, u32[]{:S(2)}) collective-permute-start(f32[64,128]{1,0:T(8,128)S(1)} %get-tuple-element.37), channel_id=1, source_target_pairs={{8,16},{24,32},{40,48},{56,64},{72,80},{88,96},{104,112},{120,128}... | collective-permute-start | bytes 98312 | tf_op jit(solution)/shard_map/ppermute | solution.py:303
  26.2 4.2 %collective-permute-start.9 = (f32[64,128]{1,0:T(8,128)S(1)}, f32[64,128]{1,0:T(8,128)S(1)}, u32[]{:S(2)}, u32[]{:S(2)}) collective-permute-start(f32[64,128]{1,0:T(8,128)S(1)} %get-tuple-element.38), channel_id=1, source_target_pairs={{1,2},{3,4},{5,6},{7,0},{2,1},{4,3},{6,5},{0,7},{9,10},{11,12},{13... | collective-permute-start | bytes 98312 | tf_op jit(solution)/shard_map/ppermute | solution.py:303
  26.2 4.2 %collective-permute-start.10 = (f32[64,128]{1,0:T(8,128)S(1)}, f32[64,128]{1,0:T(8,128)S(1)}, u32[]{:S(2)}, u32[]{:S(2)}) collective-permute-start(f32[64,128]{1,0:T(8,128)S(1)} %get-tuple-element.39), channel_id=1, source_target_pairs={{0,8},{8,0},{16,24},{24,16},{32,40},{40,32},{48,56},{56,48},{64,72... | collective-permute-start | bytes 98312 | tf_op jit(solution)/shard_map/ppermute | solution.py:303
  26.2 4.2 %collective-permute-start.11 = (f32[64,128]{1,0:T(8,128)S(1)}, f32[64,128]{1,0:T(8,128)S(1)}, u32[]{:S(2)}, u32[]{:S(2)}) collective-permute-start(f32[64,128]{1,0:T(8,128)S(1)} %get-tuple-element.40), channel_id=1, source_target_pairs={{0,1},{1,0},{2,3},{3,2},{4,5},{5,4},{6,7},{7,6},{8,9},{9,8},{10,11... | collective-permute-start | bytes 98312 | tf_op jit(solution)/shard_map/ppermute | solution.py:303
  31.8 1.3 %collective-permute-start.12 = (f32[72,128]{1,0:T(8,128)S(1)}, f32[72,128]{1,0:T(8,128)S(1)}, u32[]{:S(2)}, u32[]{:S(2)}) collective-permute-start(f32[72,128]{1,0:T(8,128)S(1)} %get-tuple-element.42), channel_id=1, source_target_pairs={{0,1},{1,0},{2,3},{3,2},{4,5},{5,4},{6,7},{7,6},{8,9},{9,8},{10,11... | collective-permute-start | bytes 110600 | tf_op jit(solution)/shard_map/ppermute | solution.py:313
  33.1 5.6 %collective-permute-start.15 = (f32[72,128]{1,0:T(8,128)S(1)}, f32[72,128]{1,0:T(8,128)S(1)}, u32[]{:S(2)}, u32[]{:S(2)}) collective-permute-start(f32[72,128]{1,0:T(8,128)S(1)} %add.30), channel_id=1, source_target_pairs={{0,4},{1,5},{2,6},{3,7},{4,0},{5,1},{6,2},{7,3},{8,12},{9,13},{10,... | collective-permute-start | bytes 110600 | tf_op jit(solution)/shard_map/ppermute | solution.py:313
  35.4 4.0 %collective-permute-start.14 = (f32[72,128]{1,0:T(8,128)S(1)}, f32[72,128]{1,0:T(8,128)S(1)}, u32[]{:S(2)}, u32[]{:S(2)}) collective-permute-start(f32[72,128]{1,0:T(8,128)S(1)} %add.30), channel_id=1, source_target_pairs={{0,6},{1,7},{2,4},{3,5},{4,2},{5,3},{6,0},{7,1},{8,14},{9,15},{10,... | collective-permute-start | bytes 110600 | tf_op jit(solution)/shard_map/ppermute | solution.py:313
  37.2 4.0 %collective-permute-start.13 = (f32[72,128]{1,0:T(8,128)S(1)}, f32[72,128]{1,0:T(8,128)S(1)}, u32[]{:S(2)}, u32[]{:S(2)}) collective-permute-start(f32[72,128]{1,0:T(8,128)S(1)} %add.30), channel_id=1, source_target_pairs={{0,2},{1,3},{2,0},{3,1},{4,6},{5,7},{6,4},{7,5},{8,10},{9,11},{10,... | collective-permute-start | bytes 110600 | tf_op jit(solution)/shard_map/ppermute | solution.py:313
  41.1 5.7 %collective-permute-start.18 = (f32[72,128]{1,0:T(8,128)S(1)}, f32[72,128]{1,0:T(8,128)S(1)}, u32[]{:S(2)}, u32[]{:S(2)}) collective-permute-start(f32[72,128]{1,0:T(8,128)S(1)} %add_add_fusion.2), channel_id=1, source_target_pairs={{0,16},{8,24},{16,0},{24,8},{32,48},{40,56},{48,32},{56,40},{64,80... | collective-permute-start | bytes 110600 | tf_op jit(solution)/shard_map/ppermute | solution.py:313
  41.2 5.7 %collective-permute-start.17 = (f32[72,128]{1,0:T(8,128)S(1)}, f32[72,128]{1,0:T(8,128)S(1)}, u32[]{:S(2)}, u32[]{:S(2)}) collective-permute-start(f32[72,128]{1,0:T(8,128)S(1)} %add_add_fusion.2), channel_id=1, source_target_pairs={{0,24},{8,16},{16,8},{24,0},{32,56},{40,48},{48,40},{56,32},{64,88... | collective-permute-start | bytes 110600 | tf_op jit(solution)/shard_map/ppermute | solution.py:313
  43.9 4.0 %collective-permute-start.16 = (f32[72,128]{1,0:T(8,128)S(1)}, f32[72,128]{1,0:T(8,128)S(1)}, u32[]{:S(2)}, u32[]{:S(2)}) collective-permute-start(f32[72,128]{1,0:T(8,128)S(1)} %add_add_fusion.2), channel_id=1, source_target_pairs={{0,8},{8,0},{16,24},{24,16},{32,40},{40,32},{48,56},{56,48},{64,72... | collective-permute-start | bytes 110600 | tf_op jit(solution)/shard_map/ppermute | solution.py:313
  47.9 5.3 %collective-permute-start.21 = (f32[72,128]{1,0:T(8,128)S(1)}, f32[72,128]{1,0:T(8,128)S(1)}, u32[]{:S(2)}, u32[]{:S(2)}) collective-permute-start(f32[72,128]{1,0:T(8,128)S(1)} %add_add_fusion.1), channel_id=1, source_target_pairs={{0,224},{8,232},{16,240},{24,248},{32,192},{40,200},{48,208},{56,2... | collective-permute-start | bytes 110600 | tf_op jit(solution)/shard_map/ppermute | solution.py:313
  48.3 6.2 %collective-permute-start.20 = (f32[72,128]{1,0:T(8,128)S(1)}, f32[72,128]{1,0:T(8,128)S(1)}, u32[]{:S(2)}, u32[]{:S(2)}) collective-permute-start(f32[72,128]{1,0:T(8,128)S(1)} %add_add_fusion.1), channel_id=1, source_target_pairs={{0,192},{8,200},{16,208},{24,216},{32,224},{40,232},{48,240},{56,2... | collective-permute-start | bytes 110600 | tf_op jit(solution)/shard_map/ppermute | solution.py:313
  49.1 6.3 %collective-permute-start.19 = (f32[72,128]{1,0:T(8,128)S(1)}, f32[72,128]{1,0:T(8,128)S(1)}, u32[]{:S(2)}, u32[]{:S(2)}) collective-permute-start(f32[72,128]{1,0:T(8,128)S(1)} %add_add_fusion.1), channel_id=1, source_target_pairs={{0,32},{8,40},{16,48},{24,56},{32,0},{40,8},{48,16},{56,24},{64,96... | collective-permute-start | bytes 110600 | tf_op jit(solution)/shard_map/ppermute | solution.py:313
  55.4 4.9 %collective-permute-start.22 = (f32[72,128]{1,0:T(8,128)S(1)}, f32[72,128]{1,0:T(8,128)S(1)}, u32[]{:S(2)}, u32[]{:S(2)}) collective-permute-start(f32[72,128]{1,0:T(8,128)S(1)} %add_add_fusion.mine), channel_id=1, source_target_pairs={{0,64},{8,72},{16,80},{24,88},{32,96},{40,104},{48,112},{56,120},{... | collective-permute-start | bytes 110600 | tf_op jit(solution)/shard_map/ppermute | solution.py:313
  (3 other events, 33.1 us)
